TPU v7x, 32 devices: a whole 2x2x4 slice. The times are simulated.
32 devices in a mesh: dp: 16 (over z, x, core), tensor: 2 (over y).
Axes of the slice: x: 2, y: 2, z: 4, core: 2. Of those that a mesh axis runs over, the one named last changes fastest.
Arguments:
- layer_input: bfloat16 [16384, 768], P(('dp', 'tensor')), may hold values from -11 to 11
- grad_out: bfloat16 [16384, 768], P(('dp', 'tensor')), may hold values from -6 to 6
- segment: int32 [16384], P('dp'), may hold values from 0 to 63, never falling along the last dimension, each value on 1 to 1024 neighbouring positions
- entity: int32 [16384], P('dp'), may hold values 0 or 1
- valid_mask: int32 [16384], P('dp'), may hold values from 0 to 1, as said below
- query_weight: bfloat16 [4, 768, 768], P(None, 'dp', 'tensor'), may hold values from -0.4375 to 0.4375
- key_value_weight: bfloat16 [2, 768, 768], P(None, 'dp', 'tensor'), may hold values from -0.21875 to 0.21875
- attn_bias: bfloat16 [5, 768], P(None, 'tensor'), may hold values from -3 to 3
- out_weight: bfloat16 [768, 768], P('tensor', 'dp'), may hold values from -0.875 to 0.875
- out_bias: bfloat16 [2, 768], replicated, may hold values from -2 to 2
- ln_gain: bfloat16 [2, 768], replicated, may hold values from 0.25 to 1.75
- ln_bias: bfloat16 [2, 768], replicated, may hold values from -2 to 2
- up_weight: bfloat16 [768, 3072], P('dp', 'tensor'), may hold values from -0.21875 to 0.21875
- ffn_bias: bfloat16 [3072], P('tensor'), may hold values from -3 to 3
- down_weight: bfloat16 [3072, 768], P('tensor', 'dp'), may hold values from -0.109375 to 0.109375
Outputs:
- output: bfloat16 [16384, 768], P(('dp', 'tensor'))
- input_grad: float32 [16384, 768], P(('dp', 'tensor'))
- residual_rms: float32 [4], replicated
- query_weight_grad: float32 [4, 768, 768], P(None, 'dp', 'tensor')
- key_value_weight_grad: float32 [2, 768, 768], P(None, 'dp', 'tensor')
- attn_bias_grad: float32 [5, 768], P(None, 'tensor')
- out_weight_grad: float32 [768, 768], P('tensor', 'dp')
- out_bias_grad: float32 [2, 768], replicated
- ln_gain_grad: float32 [2, 768], replicated
- ln_bias_grad: float32 [2, 768], replicated
- up_weight_grad: float32 [768, 3072], P('dp', 'tensor')
- ffn_bias_grad: float32 [3072], P('tensor')
- down_weight_grad: float32 [3072, 768], P('tensor', 'dp')
Inputs may be any that keep to these rules, and one draw needn't show every extreme that they name: segment numbers never fall along the tokens. `valid_mask`: the first token of every sequence of 1024 tokens is real.
All inputs are finite; a program needn't handle non-finite values. No bound on the sum of `entity` on one device may be relied on, other than what follows from the above.
Results may differ from a plain program's by a relative error of at most 0.017.
Values may be sent and summed in bfloat16 or wider, within the bound.
A program may use at most 128 MiB of HBM per device.

v0:
```python
import functools

import jax
import jax.numpy as jnp
from jax import lax
from jax.experimental import pallas as pl
from jax.experimental.pallas import tpu as pltpu
from jax.sharding import PartitionSpec as P

HEAD = 64
EPS = 1e-06
NEG = -1e30
GRID = 16
LANES = 128
MESH = pl.DeviceIdType.MESH
BF16 = jnp.bfloat16
F32 = jnp.float32
VMEM_LIMIT = 60 * 1024 * 1024


BLOCK = 512
TAIL = 0.34
TAIL_Q = (
    0.1918165616711201,
    0.1920366827922902,
    0.17827181747742213,
    0.1748548010854969,
    0.05944614604180367,
    0.27541659722682194,
    -0.27820700083503797,
    0.4016320911891782,
    -0.24597742961536673,
    0.050709736470982834,
)


def gelu_pair(v):
    size = jnp.abs(v)
    t = 1.0 / (1.0 + (TAIL * 0.5**0.5) * size)
    q = jnp.full_like(v, TAIL_Q[-1])
    for coefficient in TAIL_Q[-2::-1]:
        q = q * t + coefficient
    bell = jnp.exp(-0.5 * (v * v))
    tail = 0.5 * (bell * (t * q))
    cdf = jnp.where(v < 0, tail, 1.0 - tail)
    return v * cdf, cdf + v * (bell * 0.3989422804014327)


def normalize(resid):
    center = resid - jnp.mean(resid, -1, keepdims=True)
    inverse = lax.rsqrt(jnp.mean(center * center, -1, keepdims=True) + EPS)
    return center * inverse, inverse


def norm_backward(grad, normal, inverse, gain):
    scaled = grad * gain
    return inverse * (
        scaled
        - jnp.mean(scaled, -1, keepdims=True)
        - normal * jnp.mean(scaled * normal, -1, keepdims=True)
    )


def column_sum(a):
    return jnp.sum(a, 0, keepdims=True)


class Place:
    def __init__(self, subs):
        rank = lax.axis_index("dp")
        self.subs = subs
        self.sub = rank % subs
        block = rank // subs
        self.z = block // 4
        self.x = (block // 2) % 2
        self.c = block % 2
        self.y = lax.axis_index("tensor")
        self.moved = self.y != self.c
        self.x1 = jnp.where(self.c == 0, 1 - self.x, self.x)
        self.y1 = jnp.where(self.c == 0, self.y, 1 - self.y)
        self.x2 = jnp.where(self.c == 0, self.x, 1 - self.x)
        self.y2 = jnp.where(self.c == 0, 1 - self.y, self.y)

    def device(self, z=None, x=None, c=None, y=None):
        z = self.z if z is None else z
        x = self.x if x is None else x
        c = self.c if c is None else c
        y = self.y if y is None else y
        return (((z * 2 + x) * 2 + c) * self.subs + self.sub, y)

    def z_peer(self, step):
        return self.device(z=(self.z + step) % 4)

    def first(self):
        return self.device(x=self.x1, y=self.y1)

    def second(self):
        return self.device(x=self.x2, y=self.y2)

    def sibling(self):
        return self.device(c=1 - self.c)

    def across(self):
        return self.device(y=1 - self.y)

    def transposed(self):
        return self.device(c=1 - self.c, y=1 - self.y)

    def pieces(self):
        return (
            (self.x, self.y),
            (self.x1, self.y1),
            (self.x2, self.y2),
            (1 - self.x, 1 - self.y),
        )


def entry_barrier(place):
    barrier = pltpu.get_barrier_semaphore()
    peers = [place.z_peer(step) for step in (1, 2, 3)]
    peers += [place.device(x=1 - place.x), place.across(), place.sibling(), place.transposed()]
    for peer in peers:
        pl.semaphore_signal(barrier, inc=1, device_id=peer, device_id_type=MESH)
    pl.semaphore_wait(barrier, len(peers))


def remote(src, dst, send, recv, peer):
    return pltpu.make_async_remote_copy(
        src_ref=src, dst_ref=dst, send_sem=send, recv_sem=recv, device_id=peer, device_id_type=MESH
    )


class Gather:
    def __init__(self, place, shard, full, send, recv, local=None, whole=True):
        self.place, self.shard, self.full, self.whole = place, shard, full, whole
        self.send, self.recv, self.local = send, recv, local
        self.w = full.shape[-1] // 2

    def cols(self, y):
        return pl.ds(pl.multiple_of(y * self.w, LANES), self.w)

    def piece(self, spot, c):
        x, y = spot
        return self.full.at[:, :, x, c, :, self.cols(y)]

    def copy(self, index, src, dst, peer):
        remote(src, dst, self.send.at[index], self.recv.at[index], peer).start()

    def arrive(self, index, ref):
        remote(ref, ref, self.send.at[index], self.recv.at[index], self.place.sibling()).wait_recv()

    def gone(self, index, ref):
        remote(ref, ref, self.send.at[index], self.recv.at[index], self.place.sibling()).wait_send()

    def own(self, z):
        p = self.place
        return self.full.at[:, z, p.x, p.c, :, self.cols(p.y)]

    def stage1(self):
        p = self.place
        self.kept = pltpu.make_async_copy(self.shard, self.own(p.z), self.local)
        self.kept.start()
        for step in (1, 2, 3):
            self.copy(step - 1, self.shard, self.own(p.z), p.z_peer(step))

    def land(self):
        p = self.place
        self.kept.wait()
        for step in (1, 2, 3):
            self.arrive(step - 1, self.own((p.z + 4 - step) % 4))

    def settle(self):
        self.land()
        for index in range(3):
            self.gone(index, self.shard)

    def spread(self):
        p = self.place
        mine = self.piece(p.pieces()[0], p.c)
        self.copy(3, mine, mine, p.first())
        self.copy(4, mine, mine, p.second())
        self.copy(6, mine, mine, p.sibling())

    def stage2(self):
        self.land()
        self.spread()

    def stage3(self):
        p = self.place
        got = self.piece(p.pieces()[1], p.c)
        self.arrive(3, got)
        self.copy(5, got, got, p.second())
        self.copy(7, got, got, p.sibling())

    def stage4(self):
        p = self.place
        for index, spot in ((4, 2), (5, 3)):
            got = self.piece(p.pieces()[spot], p.c)
            self.arrive(index, got)
            self.copy(index + 4, got, got, p.sibling())

    def stage5(self):
        p = self.place
        spots = p.pieces()
        for index, spot in ((6, 0), (7, 2), (8, 1), (9, 3)):
            self.arrive(index, self.piece(spots[spot], 1 - p.c))
        for index in range(3, 10):
            self.gone(index, self.piece(spots[0], p.c))

    def last(self):
        self.stage5()
        for index in range(3):
            self.gone(index, self.shard)

    def stages(self):
        if not self.whole:
            return [self.stage1, self.settle]
        return [self.stage1, self.stage2, self.stage3, self.stage4, self.last]


def wavefront(movers):
    lists = [mover.stages() for mover in movers]
    depth = max(len(stages) for stages in lists)
    order = []
    for time in range(len(lists) + depth - 1):
        for index in range(len(lists)):
            stage = time - index
            if 0 <= stage < len(lists[index]):
                order.append(lists[index][stage])
    return order


class Share:
    def __init__(self, source, pair, index, peer, sems):
        self.kept = pltpu.make_async_copy(source, pair.at[index], sems.at[2])
        self.sent = remote(source, pair.at[index], sems.at[0], sems.at[1], peer)

    def start(self):
        self.kept.start()
        self.sent.start()

    def finish(self):
        self.kept.wait()
        self.sent.wait()


class Rows:
    def __init__(self, place, rows, both, sems):
        p = place
        half = both.at[p.c]
        self.moved = p.moved
        self.kept = pltpu.make_async_copy(rows, half, sems.at[4])
        self.swap = remote(rows, both.at[p.y], sems.at[0], sems.at[1], p.transposed())
        self.swapped = remote(half, half, sems.at[0], sems.at[1], p.transposed())
        self.share = remote(rows, half, sems.at[2], sems.at[3], p.sibling())
        self.relay = remote(half, half, sems.at[2], sems.at[3], p.sibling())
        other = both.at[1 - p.c]
        self.other = remote(other, other, sems.at[2], sems.at[3], p.sibling())

    def start(self):
        @pl.when(self.moved)
        def _():
            self.swap.start()

        @pl.when(jnp.logical_not(self.moved))
        def _():
            self.kept.start()
            self.share.start()

    def forward(self):
        @pl.when(self.moved)
        def _():
            self.swapped.wait_recv()
            self.relay.start()

    def finish(self):
        @pl.when(self.moved)
        def _():
            self.swap.wait_send()
            self.relay.wait_send()

        @pl.when(jnp.logical_not(self.moved))
        def _():
            self.kept.wait()
            self.share.wait_send()

        self.other.wait_recv()


def gather_kernel(subs, count, wholes, *refs):
    shards, (rows, bias, facts) = refs[:count], refs[count : count + 3]
    fulls, (both, biases, pair_facts) = refs[count + 3 : 2 * count + 3], refs[2 * count + 3 : 2 * count + 6]
    send, recv, local, row_sems, share_sems = refs[2 * count + 6 :]
    place = Place(subs)
    entry_barrier(place)
    tokens = Rows(place, rows, both, row_sems)
    shares = [
        Share(facts, pair_facts, place.c, place.sibling(), share_sems.at[0]),
        Share(bias, biases, place.y, place.across(), share_sems.at[1]),
    ]
    tokens.start()
    for share in shares:
        share.start()
    movers = [
        Gather(place, shards[i], fulls[i], send.at[i], recv.at[i], local.at[i], i < wholes)
        for i in range(count)
    ]
    for mover in movers:
        mover.stage1()
    for index, step in enumerate(wavefront(movers)):
        if step.__func__ is not Gather.stage1:
            step()
        if index == count:
            tokens.forward()
    tokens.finish()
    for share in shares:
        share.finish()


def gather_weights(subs, shards, wholes, rows, bias, facts):
    count = len(shards)
    outs = [
        jax.ShapeDtypeStruct((s.shape[0], 4, 2, 2, s.shape[1], 2 * s.shape[2]), BF16) for s in shards
    ]
    outs += [jax.ShapeDtypeStruct((2,) + a.shape, a.dtype) for a in (rows, bias, facts)]
    results = pl.pallas_call(
        functools.partial(gather_kernel, subs, count, wholes),
        out_shape=outs,
        in_specs=[pl.BlockSpec(memory_space=pltpu.VMEM)] * (count + 3),
        out_specs=[pl.BlockSpec(memory_space=pl.ANY)] * (count + 3),
        scratch_shapes=[
            pltpu.SemaphoreType.DMA((count, 10)),
            pltpu.SemaphoreType.DMA((count, 10)),
            pltpu.SemaphoreType.DMA((count,)),
            pltpu.SemaphoreType.DMA((5,)),
            pltpu.SemaphoreType.DMA((2, 3)),
        ],
        compiler_params=pltpu.CompilerParams(
            collective_id=0, has_side_effects=True, vmem_limit_bytes=VMEM_LIMIT
        ),
        name="gather_weights",
    )(*shards, rows, bias, facts)
    return results[:count], results[count:]


def as_matrix(full):
    return full.reshape(full.shape[0], GRID * full.shape[4], full.shape[5])


class Scatter:
    def __init__(self, place, part, total, mine, from_core, from_second, from_first, from_z, send, recv, local):
        self.place, self.part, self.total = place, part, total
        self.mine, self.from_core = mine, from_core
        self.from_second, self.from_first, self.from_z = from_second, from_first, from_z
        self.send, self.recv, self.local = send, recv, local
        self.m, self.rows, self.w = total.shape
        self.started = []

    def cols(self, y):
        return pl.ds(pl.multiple_of(y * self.w, LANES), self.w)

    def copy(self, index, src, dst, peer):
        step = remote(src, dst, self.send.at[index], self.recv.at[index], peer)
        step.start()
        self.started.append(step)

    def arrive(self, index, ref):
        remote(ref, ref, self.send.at[index], self.recv.at[index], self.place.sibling()).wait_recv()

    def add(self, target, source):
        m = self.m

        def step(index, carry):
            i, z = index // 4, index % 4
            target[i, z] = (target[i, z].astype(F32) + source[i, z].astype(F32)).astype(BF16)
            return carry

        lax.fori_loop(0, m * 4, step, 0)

    def stage1(self):
        p = self.place
        spots = p.pieces()
        self.kept = []
        for slot, (here, there) in enumerate(((3, 3), (2, 1), (1, 2), (0, 0))):
            x, y = spots[here]
            keep = pltpu.make_async_copy(
                self.part.at[:, :, x, p.c, :, self.cols(y)], self.mine.at[slot], self.local.at[slot]
            )
            keep.start()
            self.kept.append(keep)
            x, y = spots[there]
            self.copy(
                slot,
                self.part.at[:, :, x, 1 - p.c, :, self.cols(y)],
                self.from_core.at[slot],
                p.sibling(),
            )

    def joined(self, slot):
        self.kept[slot].wait()
        self.arrive(slot, self.from_core.at[slot])
        self.add(self.mine.at[slot], self.from_core.at[slot])

    def stage2(self):
        p = self.place
        for slot in (0, 1):
            self.joined(slot)
            self.copy(4 + slot, self.mine.at[slot], self.from_second.at[slot], p.second())
        for slot in (2, 3):
            self.joined(slot)

    def stage3(self):
        p = self.place
        self.arrive(4, self.from_second.at[0])
        self.add(self.mine.at[2], self.from_second.at[0])
        self.copy(6, self.mine.at[2], self.from_first, p.first())
        self.arrive(5, self.from_second.at[1])
        self.add(self.mine.at[3], self.from_second.at[1])

    def stage4(self):
        p = self.place
        self.arrive(6, self.from_first)
        self.add(self.mine.at[3], self.from_first)
        for step in (1, 2, 3):
            self.copy(
                6 + step, self.mine.at[3, :, (p.z + step) % 4], self.from_z.at[step - 1], p.z_peer(step)
            )

    def stage5(self):
        p = self.place
        for step in (1, 2, 3):
            self.arrive(6 + step, self.from_z.at[step - 1])

        def step(i, carry):
            total = self.mine[3, i, p.z].astype(F32)
            for s in range(3):
                total = total + self.from_z[s, i].astype(F32)
            self.total[i] = total
            return carry

        lax.fori_loop(0, self.m, step, 0)
        for step in self.started:
            step.wait_send()

    def stages(self):
        return [self.stage1, self.stage2, self.stage3, self.stage4, self.stage5]


class Sum:
    def __init__(self, place, source, total, box, send, recv):
        self.place, self.source, self.total = place, source, total
        self.box, self.send, self.recv = box, send, recv

    def hop(self, index):
        p = self.place
        flip = p.z + 1 - 2 * (p.z % 2)
        far = (p.z + 2) % 4
        peers = (p.sibling(), p.device(x=1 - p.x), p.device(y=1 - p.y), p.device(z=flip), p.device(z=far))
        if index < 5:
            src = self.source if index == 0 else self.total.at[index - 1]
            step = remote(src, self.box.at[index], self.send.at[index], self.recv.at[index], peers[index])
            step.start()
            self.flying = step

    def land(self, index):
        self.flying.wait()
        src = self.source if index == 0 else self.total.at[index - 1]
        self.total[index] = src[...] + self.box[index]

    def stages(self):
        def first():
            self.hop(0)

        def later(index):
            self.land(index)
            self.hop(index + 1)

        return [first] + [functools.partial(later, i) for i in range(5)]


def scatter_scratch(shape):
    m, rows, w = shape
    return [
        pltpu.VMEM((4, m, 4, rows, w), BF16),
        pltpu.VMEM((4, m, 4, rows, w), BF16),
        pltpu.VMEM((2, m, 4, rows, w), BF16),
        pltpu.VMEM((m, 4, rows, w), BF16),
        pltpu.VMEM((3, m, rows, w), BF16),
        pltpu.SemaphoreType.DMA((10,)),
        pltpu.SemaphoreType.DMA((10,)),
        pltpu.SemaphoreType.DMA((4,)),
    ]


def scatter_kernel(subs, count, *refs):
    parts, small = refs[:count], refs[count]
    totals, small_total = refs[count + 1 : 2 * count + 1], refs[2 * count + 1]
    scratch = refs[2 * count + 2 :]
    place = Place(subs)
    entry_barrier(place)
    movers = [
        Scatter(place, parts[i], totals[i], *scratch[8 * i : 8 * i + 8]) for i in range(count)
    ]
    running, box, send, recv = scratch[8 * count :]
    small_sum = Sum(place, small, running, box, send, recv)
    for mover in movers:
        mover.stage1()
    steps = [s for s in wavefront(movers) if s.__func__ is not Scatter.stage1]
    extra = small_sum.stages()
    for index, step in enumerate(steps):
        if index < len(extra):
            extra[index]()
        step()
    for step in extra[len(steps) :]:
        step()
    small_total[...] = running[4]


def scatter_gradients(subs, parts, small):
    count = len(parts)
    rows = parts[0].shape[1] // GRID
    shaped = [p.reshape(p.shape[0], 4, 2, 2, rows, p.shape[2]) for p in parts]
    shapes = [(p.shape[0], rows, p.shape[2] // 2) for p in parts]
    outs = [jax.ShapeDtypeStruct(s, F32) for s in shapes]
    outs.append(jax.ShapeDtypeStruct(small.shape, F32))
    scratch = []
    for s in shapes:
        scratch += scatter_scratch(s)
    scratch += [
        pltpu.VMEM((5,) + small.shape, F32),
        pltpu.VMEM((5,) + small.shape, F32),
        pltpu.SemaphoreType.DMA((5,)),
        pltpu.SemaphoreType.DMA((5,)),
    ]
    results = pl.pallas_call(
        functools.partial(scatter_kernel, subs, count),
        out_shape=outs,
        in_specs=[pl.BlockSpec(memory_space=pl.ANY)] * count + [pl.BlockSpec(memory_space=pltpu.VMEM)],
        out_specs=[pl.BlockSpec(memory_space=pltpu.VMEM)] * (count + 1),
        scratch_shapes=scratch,
        compiler_params=pltpu.CompilerParams(
            collective_id=1, has_side_effects=True, vmem_limit_bytes=VMEM_LIMIT
        ),
        name="scatter_gradients",
    )(*shaped, small)
    return results[:count], results[count]


def head_lanes(half):
    lane = lax.broadcasted_iota(jnp.int32, (1, LANES), 1)
    return (lane // HEAD) == half


def dot_nt(a, b):
    return lax.dot_general(a, b, (((1,), (1,)), ((), ())), preferred_element_type=F32)


def dot_nn(a, b):
    return lax.dot_general(a, b, (((1,), (0,)), ((), ())), preferred_element_type=F32)


def forward_kernel(
    subs, both, wq, wkv, biases, facts, up_in, down_in,
    ctx, probs, word, entity, keys, values, up, down, mask, column, send, recv,
):
    place = Place(subs)
    step = pl.program_id(0)
    length, rows = mask.shape
    movers = [Gather(place, None, full, send.at[i], recv.at[i]) for i, full in enumerate((up, down))]
    own = pl.ds(pl.multiple_of(place.c * rows, LANES), rows)

    @pl.when(step == 0)
    def _():
        entry_barrier(place)
        for mover in movers:
            mover.spread()
        column[...] = facts[place.y].T
        spot = lax.broadcasted_iota(jnp.int32, (length, rows), 0)
        here = lax.broadcasted_iota(jnp.int32, (length, rows), 1) + place.c * rows
        same = column[:, 0:1] == facts[place.y, 0:1, own]
        seen = (column[:, 2:3] == 1) | (spot == here)
        mask[...] = jnp.where(same & seen, 0.0, NEG)

    @pl.when(step == 3)
    def _():
        movers[0].stage3()

    @pl.when(step == 5)
    def _():
        movers[1].stage3()

    tokens = both[...].reshape(length, both.shape[2])
    mine = both[place.c]
    bias = biases[0]
    row_ent = column[own, 1:2] == 1
    to_word = dot_nn(mine, jnp.concatenate([wq[0], wq[2]], axis=1))
    to_ent = dot_nn(mine, jnp.concatenate([wq[1], wq[3]], axis=1))
    scale = HEAD ** (-0.5)
    query_word = jnp.where(row_ent, to_word[:, LANES:] + bias[2:3], to_word[:, :LANES] + bias[0:1])
    query_ent = jnp.where(row_ent, to_ent[:, LANES:] + bias[3:4], to_ent[:, :LANES] + bias[1:2])
    word[...] = query_word.astype(BF16) * BF16(scale)
    entity[...] = query_ent.astype(BF16) * BF16(scale)
    pair = dot_nn(tokens, jnp.concatenate([wkv[0], wkv[1]], axis=1))
    key = pair[:, :LANES].astype(BF16)
    value = (pair[:, LANES:] + bias[4:5]).astype(BF16)
    keys[...] = key
    values[...] = value

    queries = jnp.concatenate([word[...], entity[...]], axis=1)
    ent = column[:, 1:2] == 1
    zero = jnp.zeros_like(key)
    turned = value.T
    for half in range(2):
        lanes = head_lanes(half)
        wide = jnp.concatenate(
            [jnp.where(lanes & ~ent, key, zero), jnp.where(lanes & ent, key, zero)], axis=1
        )
        scores = dot_nt(wide, queries) + mask[...]
        top = jnp.max(scores, axis=0, keepdims=True)
        expo = jnp.exp(scores - top)
        total = jnp.sum(expo, axis=0, keepdims=True)
        prob = (expo * (1.0 / total)).astype(BF16)
        probs[half] = prob
        ctx[half * HEAD : (half + 1) * HEAD, :] = dot_nn(
            turned[half * HEAD : (half + 1) * HEAD, :], prob
        ).astype(BF16)

    @pl.when(step == pl.num_programs(0) - 1)
    def _():
        for mover in movers:
            mover.stage4()
        for mover in movers:
            mover.stage5()


def attention_forward(subs, both, wq, wkv, biases, facts, up, down):
    _, rows, width = both.shape
    length = 2 * rows
    pairs = width // LANES
    span = biases.shape[2] // LANES
    block = lambda n: pl.BlockSpec((n, LANES), lambda i: (0, i))
    whole = lambda a: pl.BlockSpec(a.shape, lambda i: (0,) * a.ndim, pipeline_mode=pl.Buffered(1))
    cols = lambda a: pl.BlockSpec(a.shape[:2] + (LANES,), lambda i: (0, 0, i))
    anywhere = pl.BlockSpec(memory_space=pl.ANY)
    return pl.pallas_call(
        functools.partial(forward_kernel, subs),
        grid=(pairs,),
        out_shape=[
            jax.ShapeDtypeStruct((width, rows), BF16),
            jax.ShapeDtypeStruct((2 * pairs, length, rows), BF16),
            jax.ShapeDtypeStruct((rows, width), BF16),
            jax.ShapeDtypeStruct((rows, width), BF16),
            jax.ShapeDtypeStruct((length, width), BF16),
            jax.ShapeDtypeStruct((length, width), BF16),
            jax.ShapeDtypeStruct(up.shape, BF16),
            jax.ShapeDtypeStruct(down.shape, BF16),
        ],
        in_specs=[
            whole(both),
            cols(wq),
            cols(wkv),
            pl.BlockSpec((1, biases.shape[1], LANES), lambda i: (i // span, 0, i % span)),
            whole(facts),
            anywhere,
            anywhere,
        ],
        out_specs=[
            pl.BlockSpec((LANES, rows), lambda i: (i, 0)),
            pl.BlockSpec((2, length, rows), lambda i: (i, 0, 0)),
            block(rows),
            block(rows),
            block(length),
            block(length),
            anywhere,
            anywhere,
        ],
        scratch_shapes=[
            pltpu.VMEM((length, rows), F32),
            pltpu.VMEM((length, facts.shape[1]), jnp.int32),
            pltpu.SemaphoreType.DMA((2, 10)),
            pltpu.SemaphoreType.DMA((2, 10)),
        ],
        input_output_aliases={5: 6, 6: 7},
        compiler_params=pltpu.CompilerParams(
            collective_id=2, has_side_effects=True, vmem_limit_bytes=VMEM_LIMIT
        ),
        name="attention_forward",
    )(both, wq, wkv, biases, facts, up, down)


def backward_kernel(probs, qw, qe, keys, values, ctx, dctx, ent_col, ent_row, dqw, dqe, dkeys, dvalues):
    queries = jnp.concatenate([qw[...], qe[...]], axis=1)
    value = values[...]
    turned = keys[...].T
    ent = ent_col[...] == 1
    ent_lane = ent_row[...] == 1
    grad = dctx[...]
    zero = jnp.zeros_like(value)
    dk, dv = [], []
    for half in range(2):
        lanes = head_lanes(half)
        here = slice(half * HEAD, (half + 1) * HEAD)
        prob = probs[half]
        delta = jnp.sum(
            ctx[here, :].astype(F32) * grad[here, :].astype(F32), axis=0, keepdims=True
        )
        dprob = dot_nn(jnp.where(lanes, value, zero), grad)
        dscore = (prob.astype(F32) * (dprob - delta)).astype(BF16)
        key_t = turned[here, :]
        none = jnp.zeros_like(key_t)
        tall = jnp.concatenate(
            [jnp.where(ent_lane, none, key_t), jnp.where(ent_lane, key_t, none)], axis=0
        )
        dq = dot_nn(tall, dscore) * (HEAD ** (-0.5))
        dqw[here, :] = dq[:HEAD].astype(BF16)
        dqe[here, :] = dq[HEAD:].astype(BF16)
        both = dot_nn(dscore, queries)
        dk.append(jnp.where(ent, both[:, LANES:], both[:, :LANES]))
        dv.append(dot_nt(prob, grad))
    dkeys[...] = jnp.where(head_lanes(0), dk[0], dk[1]).astype(BF16)
    dvalues[...] = jnp.where(head_lanes(0), dv[0], dv[1]).astype(BF16)


def attention_backward(probs, qw, qe, keys, values, ctx, dctx, ent_col, ent_row):
    rows, width = qw.shape
    length = keys.shape[0]
    pairs = width // LANES
    block = lambda n: pl.BlockSpec((n, LANES), lambda i: (0, i))
    turned = pl.BlockSpec((LANES, rows), lambda i: (i, 0))
    whole = lambda a: pl.BlockSpec(a.shape, lambda i: (0,) * a.ndim)
    return pl.pallas_call(
        backward_kernel,
        grid=(pairs,),
        out_shape=[
            jax.ShapeDtypeStruct((width, rows), BF16),
            jax.ShapeDtypeStruct((width, rows), BF16),
            jax.ShapeDtypeStruct((length, width), BF16),
            jax.ShapeDtypeStruct((length, width), BF16),
        ],
        in_specs=[
            pl.BlockSpec((2, length, rows), lambda i: (i, 0, 0)),
            block(rows),
            block(rows),
            block(length),
            block(length),
            turned,
            turned,
            whole(ent_col),
            whole(ent_row),
        ],
        out_specs=[turned, turned, block(length), block(length)],
        compiler_params=pltpu.CompilerParams(vmem_limit_bytes=VMEM_LIMIT),
        name="attention_backward",
    )(probs, qw, qe, keys, values, ctx, dctx, ent_col, ent_row)


def ffn_forward_kernel(
    subs, both, ctx, w_out, up, down, unit_bias, out_bias, gain, shift, valid, grad_out,
    active, slope, hidden_low, normal_one, inverse_one, output, d_two, sums, hidden, total,
):
    step = pl.program_id(0)
    place = Place(subs)

    @pl.when(step == 0)
    def _():
        attn = dot_nt(ctx[...].T, w_out[...]) + out_bias[0:1].astype(F32)
        resid = both[place.c].astype(F32) + attn
        normal, inverse = normalize(resid)
        out = normal * gain[0:1].astype(F32) + shift[0:1].astype(F32)
        hidden[...] = out
        hidden_low[...] = out.astype(BF16)
        normal_one[...] = normal
        inverse_one[...] = inverse
        total[...] = jnp.zeros_like(total)
        seen = valid[...]
        sums[0:1] = column_sum(seen * resid * resid)
        sums[1:2] = column_sum(seen * attn * attn)

    pre = dot_nn(hidden_low[...], up[...]) + unit_bias[...]
    act, rise = gelu_pair(pre)
    act = act.astype(BF16)
    active[...] = act
    slope[...] = rise.astype(BF16)
    total[...] += dot_nt(act, down[...])

    @pl.when(step == pl.num_programs(0) - 1)
    def _():
        ffn = total[...] + out_bias[1:2].astype(F32)
        resid = hidden[...] + ffn
        normal, inverse = normalize(resid)
        output[...] = (normal * gain[1:2].astype(F32) + shift[1:2].astype(F32)).astype(BF16)
        seen = valid[...]
        grad = grad_out[...].astype(F32)
        back = norm_backward(grad, normal, inverse, gain[1:2].astype(F32))
        d_two[...] = back
        sums[2:3] = column_sum(seen * ffn * ffn)
        sums[3:4] = column_sum(seen * resid * resid)
        sums[4:5] = column_sum(grad * normal)
        sums[5:6] = column_sum(grad)
        sums[6:7] = column_sum(back.astype(BF16).astype(F32))
        sums[7:8] = jnp.zeros_like(sums[7:8]) + jnp.sum(seen) * (1.0 / seen.shape[0])


def ffn_forward(subs, both, ctx, w_out, up, down, unit_bias, out_bias, gain, shift, valid, grad_out):
    _, rows, width = both.shape
    units = up.shape[1]
    whole = lambda a: pl.BlockSpec(a.shape, lambda i: (0,) * a.ndim, pipeline_mode=pl.Buffered(1))
    fixed = lambda r, w: pl.BlockSpec((r, w), lambda i: (0, 0), pipeline_mode=pl.Buffered(1))
    wide = lambda r: pl.BlockSpec((r, BLOCK), lambda i: (0, i))
    return pl.pallas_call(
        functools.partial(ffn_forward_kernel, subs),
        grid=(units // BLOCK,),
        out_shape=[
            jax.ShapeDtypeStruct((rows, units), BF16),
            jax.ShapeDtypeStruct((rows, units), BF16),
            jax.ShapeDtypeStruct((rows, width), BF16),
            jax.ShapeDtypeStruct((rows, width), F32),
            jax.ShapeDtypeStruct((rows, 1), F32),
            jax.ShapeDtypeStruct((rows, width), BF16),
            jax.ShapeDtypeStruct((rows, width), F32),
            jax.ShapeDtypeStruct((8, width), F32),
        ],
        in_specs=[whole(both), whole(ctx), whole(w_out), wide(width), wide(width), wide(1)]
        + [whole(a) for a in (out_bias, gain, shift, valid, grad_out)],
        out_specs=[
            wide(rows),
            wide(rows),
            fixed(rows, width),
            fixed(rows, width),
            fixed(rows, 1),
            fixed(rows, width),
            fixed(rows, width),
            fixed(8, width),
        ],
        scratch_shapes=[pltpu.VMEM((rows, width), F32), pltpu.VMEM((rows, width), F32)],
        compiler_params=pltpu.CompilerParams(vmem_limit_bytes=VMEM_LIMIT),
        cost_estimate=pl.CostEstimate(
            flops=2 * rows * width * (width + 2 * units),
            bytes_accessed=2 * width * (width + 2 * units) + 4 * rows * units,
            transcendentals=rows * units,
        ),
        name="ffn_forward",
    )(both, ctx, w_out, up, down, unit_bias, out_bias, gain, shift, valid, grad_out)


def ffn_backward_kernel(
    d_two, hidden_low, active, slope, up, down, ctx, w_out, gain, normal_one, inverse_one,
    up_part, down_part, bias_part, d_one, d_ctx, out_part, sums, d_low, d_turned, hidden_turned, total,
):
    step = pl.program_id(0)

    @pl.when(step == 0)
    def _():
        low = d_two[...].astype(BF16)
        d_low[...] = low
        d_turned[...] = low.T
        hidden_turned[...] = hidden_low[...].T
        total[...] = d_two[...]

    d_pre = (dot_nn(d_low[...], down[...]) * slope[...].astype(F32)).astype(BF16)
    bias_part[...] = column_sum(d_pre.astype(F32))
    up_part[...] = dot_nn(hidden_turned[...], d_pre).astype(BF16)
    down_part[...] = dot_nn(d_turned[...], active[...]).astype(BF16)
    total[...] += dot_nt(d_pre, up[...])

    @pl.when(step == pl.num_programs(0) - 1)
    def _():
        grad = total[...]
        normal = normal_one[...]
        back = norm_backward(grad, normal, inverse_one[...], gain[0:1].astype(F32))
        d_one[...] = back
        low = back.astype(BF16)
        d_ctx[...] = dot_nt(w_out[...].T, low).astype(BF16)
        out_part[...] = dot_nt(low.T, ctx[...]).astype(BF16)
        sums[...] = jnp.zeros_like(sums)
        sums[0:1] = column_sum(grad * normal)
        sums[1:2] = column_sum(grad)
        sums[2:3] = column_sum(low.astype(F32))


def ffn_backward(d_two, hidden_low, active, slope, up, down, ctx, w_out, gain, normal_one, inverse_one):
    rows, width = d_two.shape
    units = up.shape[1]
    whole = lambda a: pl.BlockSpec(a.shape, lambda i: (0,) * a.ndim, pipeline_mode=pl.Buffered(1))
    fixed = lambda r, w: pl.BlockSpec((r, w), lambda i: (0, 0), pipeline_mode=pl.Buffered(1))
    wide = lambda r: pl.BlockSpec((r, BLOCK), lambda i: (0, i))
    return pl.pallas_call(
        ffn_backward_kernel,
        grid=(units // BLOCK,),
        out_shape=[
            jax.ShapeDtypeStruct((width, units), BF16),
            jax.ShapeDtypeStruct((width, units), BF16),
            jax.ShapeDtypeStruct((1, units), F32),
            jax.ShapeDtypeStruct((rows, width), F32),
            jax.ShapeDtypeStruct((width, rows), BF16),
            jax.ShapeDtypeStruct((width, width), BF16),
            jax.ShapeDtypeStruct((8, width), F32),
        ],
        in_specs=[whole(d_two), whole(hidden_low), wide(rows), wide(rows), wide(width), wide(width)]
        + [whole(a) for a in (ctx, w_out, gain, normal_one, inverse_one)],
        out_specs=[
            wide(width),
            wide(width),
            wide(1),
            fixed(rows, width),
            fixed(width, rows),
            fixed(width, width),
            fixed(8, width),
        ],
        scratch_shapes=[
            pltpu.VMEM((rows, width), BF16),
            pltpu.VMEM((width, rows), BF16),
            pltpu.VMEM((width, rows), BF16),
            pltpu.VMEM((rows, width), F32),
        ],
        compiler_params=pltpu.CompilerParams(vmem_limit_bytes=VMEM_LIMIT),
        cost_estimate=pl.CostEstimate(
            flops=4 * rows * width * (width + 2 * units),
            bytes_accessed=2 * width * (3 * width + 4 * units) + 4 * rows * units,
            transcendentals=0,
        ),
        name="ffn_backward",
    )(d_two, hidden_low, active, slope, up, down, ctx, w_out, gain, normal_one, inverse_one)


def body(
    layer_input,
    grad_out,
    segment,
    entity,
    valid_mask,
    query_weight,
    key_value_weight,
    attn_bias,
    out_weight,
    out_bias,
    ln_gain,
    ln_bias,
    up_weight,
    ffn_bias,
    down_weight,
):
    rows, width = layer_input.shape
    length = segment.shape[0]
    rank = lax.axis_index("tensor")
    subs = lax.axis_size("dp") // GRID
    core = (lax.axis_index("dp") // subs) % 2
    moved = rank != core
    start = core * rows
    pairs = lax.axis_size("tensor")
    trades = []
    for d in range(lax.axis_size("dp")):
        other = d + subs if (d // subs) % 2 == 0 else d - subs
        y = 1 - (d // subs) % 2
        trades.append((d * pairs + y, other * pairs + 1 - y))
    siblings = [
        (d, d + subs if (d // subs) % 2 == 0 else d - subs) for d in range(lax.axis_size("dp"))
    ]

    def trade(own):
        got = lax.ppermute(own, ("dp", "tensor"), trades)
        return jnp.where(moved, got, own)

    shards = [
        query_weight,
        key_value_weight,
        out_weight.T[None],
        up_weight[None],
        down_weight.T[None],
    ]
    groups = [[b * subs + s for s in range(subs)] for b in range(GRID)]
    if subs > 1:
        shards = [
            lax.all_gather(s, "dp", axis=1, tiled=True, axis_index_groups=groups) for s in shards
        ]
    shards = [shards[1], shards[0]] + shards[2:]
    units = pairs * ffn_bias.shape[0]
    cols = attn_bias.shape[1]
    bias_rows = jnp.concatenate([attn_bias, ffn_bias.reshape(-1, cols)]).astype(F32)
    used = bias_rows.shape[0]
    bias_rows = jnp.pad(bias_rows, ((0, -used % 16), (0, 0)))
    facts = jnp.pad(jnp.stack([segment, entity, valid_mask]), ((0, 5), (0, 0)))
    (w_kv, w_q, w_out_t, w_up, w_down_t), (both, biases, pair_facts) = gather_weights(
        subs, shards, 3, layer_input, bias_rows, facts
    )
    w_kv, w_q, w_out_t = as_matrix(w_kv), as_matrix(w_q), as_matrix(w_out_t)[0]
    context_t, probs, query_word, query_ent, keys, values, w_up, w_down_t = attention_forward(
        subs, both, w_q, w_kv, biases, pair_facts, w_up, w_down_t
    )
    w_up, w_down_t = as_matrix(w_up)[0], as_matrix(w_down_t)[0]
    ffn_bias_full = biases[:, 5:used].reshape(units)
    facts = lax.dynamic_index_in_dim(pair_facts, rank, 0, keepdims=False)
    segment, entity, valid_mask = facts[0], facts[1], facts[2]
    layer_input = lax.dynamic_index_in_dim(both, core, 0, keepdims=False)

    ent_own = lax.dynamic_slice_in_dim(entity, start, rows)
    valid_own = lax.dynamic_slice_in_dim(valid_mask, start, rows).astype(F32)[:, None]
    ent_col = entity[:, None]
    ent_row = entity[None, :]

    grad_out, context_t = lax.optimization_barrier((grad_out, context_t))
    active, slope, hidden_low, normal_one, inverse_one, result, d_two, sums_two = ffn_forward(
        subs, both, context_t, w_out_t, w_up, w_down_t, ffn_bias_full[None], out_bias, ln_gain, ln_bias, valid_own,
        trade(grad_out),
    )
    output = trade(result)
    up_part, down_part, ffn_bias_part, d_one, d_context_t, out_part, sums_one = ffn_backward(
        d_two, hidden_low, active, slope, w_up, w_down_t, context_t, w_out_t, ln_gain, normal_one, inverse_one
    )

    d_word_t, d_ent_t, d_keys_all, d_values_all = attention_backward(
        probs, query_word, query_ent, keys, values, context_t, d_context_t, ent_col, ent_row
    )
    stacked = jnp.stack([d_keys_all, d_values_all]).reshape(2, 2, rows, width)
    mine = lax.dynamic_index_in_dim(stacked, core, 1, keepdims=False)
    theirs = lax.dynamic_index_in_dim(stacked, 1 - core, 1, keepdims=False)
    swapped = lax.ppermute(theirs, "dp", siblings)
    d_kv = (mine.astype(F32) + swapped.astype(F32)).astype(BF16)

    ent_lane = (ent_own == 1)[None, :]
    none = jnp.zeros_like(d_word_t)
    d_queries_t = jnp.stack(
        [
            jnp.where(ent_lane, none, d_word_t),
            jnp.where(ent_lane, none, d_ent_t),
            jnp.where(ent_lane, d_word_t, none),
            jnp.where(ent_lane, d_ent_t, none),
        ]
    )
    query_part = jnp.einsum(
        "ld,mel->mde", layer_input, d_queries_t, preferred_element_type=F32
    ).astype(BF16)
    kv_part = jnp.einsum("ld,mle->mde", layer_input, d_kv, preferred_element_type=F32).astype(BF16)
    attn_bias_part = jnp.concatenate(
        [jnp.sum(d_queries_t.astype(F32), 2), jnp.sum(d_kv[1].astype(F32), 0)[None]], 0
    )
    input_grad = (
        d_one
        + jnp.einsum("mel,mde->ld", d_queries_t, w_q, preferred_element_type=F32)
        + jnp.einsum("mle,mde->ld", d_kv, w_kv, preferred_element_type=F32)
    )
    returned = lax.ppermute(input_grad.astype(BF16), ("dp", "tensor"), trades)
    input_grad = jnp.where(moved, returned.astype(F32), input_grad)

    small = jnp.concatenate([sums_one.reshape(-1), sums_two.reshape(-1), attn_bias_part.reshape(-1), ffn_bias_part[0]])
    padded = -(-small.shape[0] // (8 * LANES)) * 8 * LANES
    small = jnp.pad(small, (0, padded - small.shape[0])).reshape(-1, LANES)
    sums, small_sum = scatter_gradients(
        subs, [down_part[None], up_part[None], out_part[None], query_part, kv_part], small
    )
    if subs > 1:
        sums = [
            lax.psum_scatter(s, "dp", scatter_dimension=1, tiled=True, axis_index_groups=groups)
            for s in sums
        ]
        small_sum = lax.psum(small_sum, "dp", axis_index_groups=groups)
    down_sum, up_sum, out_sum, query_sum, kv_sum = sums
    flat = small_sum.reshape(-1)
    norms = flat[: 16 * width].reshape(16, width)
    gains, shifts, out_biases = (jnp.stack([norms[i], norms[12 + i]]) for i in range(3))
    attn_biases = flat[16 * width : 21 * width].reshape(5, width)
    ffn_biases = flat[21 * width : 21 * width + units]
    squares = jnp.sum(norms[8:12], 1)
    real = norms[15, 0] * rows
    half = ffn_bias.shape[0]
    return (
        output,
        input_grad,
        jnp.sqrt(squares / (real * width)),
        query_sum,
        kv_sum,
        lax.dynamic_slice_in_dim(attn_biases, rank * cols, cols, 1),
        out_sum[0].T,
        out_biases,
        gains,
        shifts,
        up_sum[0],
        lax.dynamic_slice_in_dim(ffn_biases, rank * half, half, 0),
        down_sum[0].T,
    )


def solution(mesh):
    placed = (
        P(("dp", "tensor"), None),
        P(("dp", "tensor"), None),
        P("dp"),
        P("dp"),
        P("dp"),
        P(None, "dp", "tensor"),
        P(None, "dp", "tensor"),
        P(None, "tensor"),
        P("tensor", "dp"),
        P(),
        P(),
        P(),
        P("dp", "tensor"),
        P("tensor"),
        P("tensor", "dp"),
    )
    return jax.shard_map(
        body,
        mesh=mesh,
        in_specs=placed,
        out_specs=(
            P(("dp", "tensor"), None),
            P(("dp", "tensor"), None),
            P(),
            P(None, "dp", "tensor"),
            P(None, "dp", "tensor"),
            P(None, "tensor"),
            P("tensor", "dp"),
            P(),
            P(),
            P(),
            P("dp", "tensor"),
            P("tensor"),
            P("tensor", "dp"),
        ),
        check_vma=False,
    )
```

profile of v0, /device:TPU:1, one launch (start us, length us, event | category | flops | bytes accessed | tf_op | source)
XLA Modules:
  0.0 350.4 jit_solution(12239607495194781738)
XLA Ops:
  0.6 0.7 reshape.108
  1.3 0.7 pad_add_fusion
  2.1 0.6 pad.16.refs_7_
  2.7 1.3 fusion.13.refs_6_
  4.0 63.0 %gather_weights.1 = (bf16[2,4,2,2,48,768]{5,4,3,2,1,0:T(8,128)(2,1)}, bf16[4,4,2,2,48,768]{5,4,3,2,1,0:T(8,128)(2,1)}, bf16[1,4,2,2,48,768]{5,4,3,2,1,0:T(8,128)...) custom-call(bf16[2,48,384]{2,1,0:T(8,128)(2,1)} %refs_0_.1, ...), custom_call_target="tpu_custom_call" | custom-call | tf_op jit(solution)/shard_map/gather_weights/pallas_call | solution.py:326
  67.0 57.1 %attention_forward.1 = (bf16[768,512]{1,0:T(8,128)(2,1)}, bf16[12,1024,512]{2,1,0:T(8,128)(2,1)}, bf16[512,768]{1,0:T(8,128)(2,1)}, bf16[512,768]{1,0:T(8,128)(2...) custom-call(bf16[2,512,768]{2,1,0:T(8,128)(2,1)} %get-tuple-element., ...), custom_call_target="tpu_custom_call", output_to_operand_aliasing={{6}: (5, {}), {7}: (6, {})} | custom-call | tf_op jit(solution)/shard_map/attention_forward/pallas_call | solution.py:645
  124.1 2.4 collective-permute-start
  126.5 0.8 slice.80
  127.3 0.8 fusion.14
  128.1 0.9 copy.33.valid
  129.0 0.6 broadcast_in_dim_reshape.3.unit_bias
  129.6 1.4 fusion.18
  131.0 1.0 copy.34.ent_col
  132.0 0.8 compare_reduce_fusion
  132.8 4.6 %collective-permute-done = bf16[512,768]{1,0:T(8,128)(2,1)S(1)} collective-permute-done((bf16[512,768]{1,0:T(8,128)(2,1)S(1)}, bf16[512,768]{1,0:T(8,128)(2,1)S(1)}, u32[]{:S(2)}, u32[]{:S(2)}) %collective-permute-start) | collective-permute-done | bytes 786464 | tf_op jit(solution)/shard_map/ppermute | solution.py:961
  137.4 1.0 broadcast_select_fusion.1.grad_out
  138.4 22.0 %ffn_forward.1 = (bf16[512,3072]{1,0:T(8,128)(2,1)}, bf16[512,3072]{1,0:T(8,128)(2,1)}, bf16[512,768]{1,0:T(8,128)(2,1)}, f32[512,768]{1,0:T(8,128)}, f32[512,1]...) custom-call(bf16[2,512,768]{2,1,0:T(8,128)(2,1)} %get-tuple-element.56.both, ...), custom_call_target="tpu_custom_call" | custom-call | flops 5435817984 | bytes 16908288 | tf_op jit(solution)/shard_map/ffn_forward/pallas_call | solution.py:810
  160.3 20.8 %ffn_backward.1 = (bf16[768,3072]{1,0:T(8,128)(2,1)}, bf16[768,3072]{1,0:T(8,128)(2,1)}, f32[1,3072]{1,0:T(1,128)}, f32[512,768]{1,0:T(8,128)}, bf16[768,512]{1,...) custom-call(f32[512,768]{1,0:T(8,128)} %get-tuple-element.70.d_two, ...), custom_call_target="tpu_custom_call" | custom-call | flops 10871635968 | bytes 28704768 | tf_op jit(solution)/shard_map/ffn_backward/pallas_call | solution.py:887
  181.1 16.0 %attention_backward.1 = (bf16[768,512]{1,0:T(8,128)(2,1)}, bf16[768,512]{1,0:T(8,128)(2,1)}, bf16[1024,768]{1,0:T(8,128)(2,1)}, bf16[1024,768]{1,0:T(8,128)(2,1)}) custom-call(bf16[12,1024,512]{2,1,0:T(8,128)(2,1)} %get-tuple-element.77.probs, bf16[512,768]{1,0:T(8,128)(2,1)} %get-tuple-element.78.qw, bf16[512,768]{1,0:T(8,128)(2,1)} %get-tuple-element.79.qe, ...), custom_call_target="tpu_custom_call" | custom-call | tf_op jit(solution)/shard_map/attention_backward/pallas_call | solution.py:731
  197.2 2.8 fusion.2
  200.0 2.6 collective-permute-start.1
  202.6 1.1 select_bitcast_fusion.3
  203.7 1.6 convert_reduce_fusion
  205.4 6.3 %convolution_convert_fusion = bf16[4,768,768]{1,2,0:T(8,128)(2,1)} fusion(bf16[2,512,768]{2,1,0:T(8,128)(2,1)} %get-tuple-element.56.both, s32[]{:T(128)S(6)} %select_n.73, bf16[1,768,512]{2,1,0:T(8,128)(2,1)S(1)} %get-tuple-element.113, bf16[1,768,512]{2,1,0:T(8,128)(2,1)S(1)} %get-tuple-element.100, bf16[1,768,512]{2,1,0:T(8,128)(2,1)} %get-tuple-element.114, ...), kind=kOutput, calls=%fused_computation.8 | convolution fusion | flops 2422996992 | bytes 8650756 | tf_op jit(solution)/shard_map/ld,mel->mde/dot_general | solution.py:1030
  211.8 5.2 %fusion.19 = f32[512,768,1]{1,0,2:T(8,128)} fusion(bf16[4,768,768]{2,1,0:T(8,128)(2,1)S(1)} %bitcast.122, bf16[1,768,512]{2,1,0:T(8,128)(2,1)S(1)} %get-tuple-element.113, bf16[1,768,512]{2,1,0:T(8,128)(2,1)S(1)} %get-tuple-element.100, bf16[1,768,512]{2,1,0:T(8,128)(2,1)} %get-tuple-element.114, bf16[1,768,512]{2,1,0:T(8,128)(2,1)S(1)} %get-tuple-element.99), kind=kOutput, calls=%fused_computation.67 | convolution fusion | flops 2420637696 | bytes 9437184 | tf_op jit(solution)/shard_map/mel,mde->ld/dot_general | solution.py:1039
  216.9 2.2 broadcast_select_fusion
  219.2 2.0 fusion
  221.3 2.9 convolution_convert_fusion.1
  224.3 0.6 fusion.9.refs_5_
  224.9 96.0 %scatter_gradients.1 = (f32[1,48,1536]{2,1,0:T(8,128)}, f32[1,48,1536]{2,1,0:T(8,128)}, f32[1,48,384]{2,1,0:T(8,128)}, f32[4,48,384]{2,1,0:T(8,128)}, f32[2,48,384]{2,1,0:T(8,128)}, /*index=5*/f32[152,128]{1,0:T(8,128)}) custom-call(bf16[1,4,2,2,48,3072]{5,4,3,2,1,0:T(8,128)(2,1)} %bitcast.117, bf16[1,4,2,2,48,3072]{5,4,3,2,1,0:T(8,128)(2,1)} %bitcast.116, ...), custom_call_target="tpu_custom_call" | custom-call | tf_op jit(solution)/shard_map/scatter_gradients/pallas_call | solution.py:535
  320.9 0.8 slice_bitcast_fusion.2
  321.7 0.8 slice.86
  322.5 0.8 slice_bitcast_fusion
  323.3 0.7 slice.88
  324.0 4.9 %fusion.20 = (bf16[512,768]{1,0:T(8,128)(2,1)}, f32[512,768]{1,0:T(8,128)S(1)}) fusion(bf16[2,512,768]{2,1,0:T(8,128)(2,1)S(1)} %fusion, bf16[2,768,768]{2,1,0:T(8,128)(2,1)} %bitcast.129, f32[512,768]{1,0:T(8,128)} %get-tuple-element.76, f32[512,768,1]{1,0,2:T(8,128)} %fusion.19), kind=kOutput, calls=%fused_computation.68 | convolution fusion | flops 1209139200 | bytes 9437184 | tf_op jit(solution)/shard_map/mle,mde->ld/dot_general | solution.py:1040
  328.9 6.8 %collective-permute-start.3 = (bf16[512,768]{1,0:T(8,128)(2,1)}, bf16[512,768]{1,0:T(8,128)(2,1)S(1)}, u32[]{:S(2)}, u32[]{:S(2)}) collective-permute-start(bf16[512,768]{1,0:T(8,128)(2,1)} %get-tuple-element.115), channel_id=1, source_target_pairs={{1,2},{2,1},{5,6},{6,5},{9,10},{10,9},{13,14},{14,13},{17,18},{18,... | collective-permute-start | bytes 2359304 | tf_op jit(solution)/shard_map/ppermute | solution.py:1042
  335.8 0.6 pad_maximum_fusion.4
  337.8 0.7 dynamic_slice.34
  338.4 0.6 pad_maximum_fusion.3
  339.0 0.6 pad_maximum_fusion.2
  339.6 0.6 constant_dynamic-slice_fusion
  340.8 4.8 %collective-permute-done.3 = bf16[512,768]{1,0:T(8,128)(2,1)S(1)} collective-permute-done((bf16[512,768]{1,0:T(8,128)(2,1)}, bf16[512,768]{1,0:T(8,128)(2,1)S(1)}, u32[]{:S(2)}, u32[]{:S(2)}) %collective-permute-start.3) | collective-permute-done | bytes 786464 | tf_op jit(solution)/shard_map/ppermute | solution.py:1042
  345.6 1.3 convert_select_fusion
  346.9 0.7 copy.64
  347.6 0.7 copy.65
  348.3 0.6 copy.66
  348.9 0.7 copy.67
  349.6 0.7 copy.68
  (51 shorter events, 1.5 us)
Async XLA Ops:
  67.0 57.1 %copy-start.3 = (bf16[512,768]{1,0:T(8,128)(2,1)S(1)}, bf16[512,768]{1,0:T(8,128)(2,1)}, u32[]{:S(2)}) copy-start(bf16[512,768]{1,0:T(8,128)(2,1)} %param.16) | copy-start | bytes 2359300
  124.1 13.3 %collective-permute-start = (bf16[512,768]{1,0:T(8,128)(2,1)S(1)}, bf16[512,768]{1,0:T(8,128)(2,1)S(1)}, u32[]{:S(2)}, u32[]{:S(2)}) collective-permute-start(bf16[512,768]{1,0:T(8,128)(2,1)S(1)} %copy-done.3), channel_id=1, source_target_pairs={{1,2},{2,1},{5,6},{6,5},{9,10},{10,9},{13,14},{14,13},{17,18},{18,... | collective-permute-start | bytes 2359304 | tf_op jit(solution)/shard_map/ppermute | solution.py:961
  197.1 5.5 %copy-start.4 = (bf16[768,512]{1,0:T(8,128)(2,1)S(1)}, bf16[768,512]{1,0:T(8,128)(2,1)}, u32[]{:S(2)}) copy-start(bf16[768,512]{1,0:T(8,128)(2,1)} %get-tuple-element.83) | copy-start | bytes 2359300
  197.1 5.5 %copy-start.5 = (bf16[768,512]{1,0:T(8,128)(2,1)S(1)}, bf16[768,512]{1,0:T(8,128)(2,1)}, u32[]{:S(2)}) copy-start(bf16[768,512]{1,0:T(8,128)(2,1)} %get-tuple-element.84) | copy-start | bytes 2359300
  200.0 19.2 %collective-permute-start.2 = (bf16[2,512,768]{2,1,0:T(8,128)(2,1)}, bf16[2,512,768]{2,1,0:T(8,128)(2,1)}, u32[]{:S(2)}, u32[]{:S(2)}) collective-permute-start(bf16[2,512,768]{2,1,0:T(8,128)(2,1)} %fusion.2), channel_id=1, source_target_pairs={{0,2},{2,0},{4,6},{6,4},{8,10},{10,8},{12,14},{14,12},{16,18},{18,... | collective-permute-start | bytes 4718600 | tf_op jit(solution)/shard_map/ppermute | solution.py:1017
  200.0 17.0 %collective-permute-start.1 = (bf16[512,768]{1,0:T(8,128)(2,1)}, bf16[512,768]{1,0:T(8,128)(2,1)}, u32[]{:S(2)}, u32[]{:S(2)}) collective-permute-start(bf16[512,768]{1,0:T(8,128)(2,1)} %get-tuple-element.69), channel_id=1, source_target_pairs={{1,2},{2,1},{5,6},{6,5},{9,10},{10,9},{13,14},{14,13},{17,18},{18,... | collective-permute-start | bytes 2359304 | tf_op jit(solution)/shard_map/ppermute | solution.py:961
  203.7 1.6 copy-start.12
  203.7 1.7 copy-start.11
  203.7 8.0 %slice-start = ((s8[4718592]{0:T(1024)(128)(4,1)}), s8[524288]{0:T(1024)(128)(4,1)S(1)}, s32[]{:S(2)}) async-start(s8[4718592]{0:T(1024)(128)(4,1)} %bitcast.120), calls=%async_computation | async-start | bytes 1048576
  205.4 6.3 %slice-start.1 = ((s8[4718592]{0:T(1024)(128)(4,1)}), s8[4194304]{0:T(1024)(128)(4,1)S(1)}, s32[]{:S(2)}) async-start(s8[4718592]{0:T(1024)(128)(4,1)} %bitcast.120), calls=%async_computation.1 | async-start | bytes 8388608
  211.8 7.4 %copy-start.1 = (bf16[1024,768]{1,0:T(8,128)(2,1)S(1)}, bf16[1024,768]{1,0:T(8,128)(2,1)}, u32[]{:S(2)}) copy-start(bf16[1024,768]{1,0:T(8,128)(2,1)} %get-tuple-element.86) | copy-start | bytes 4718596
  216.9 2.2 copy-start
  219.2 2.2 copy-start.2
  221.3 2.9 copy-start.13
  328.9 18.0 %copy-start.8 = (f32[4,48,384]{2,1,0:T(8,128)S(1)}, f32[4,48,384]{2,1,0:T(8,128)}, u32[]{:S(2)}) copy-start(f32[4,48,384]{2,1,0:T(8,128)} %get-tuple-element.139) | copy-start | bytes 884740
  328.9 16.7 %collective-permute-start.3 = (bf16[512,768]{1,0:T(8,128)(2,1)}, bf16[512,768]{1,0:T(8,128)(2,1)S(1)}, u32[]{:S(2)}, u32[]{:S(2)}) collective-permute-start(bf16[512,768]{1,0:T(8,128)(2,1)} %get-tuple-element.115), channel_id=1, source_target_pairs={{1,2},{2,1},{5,6},{6,5},{9,10},{10,9},{13,14},{14,13},{17,18},{18,... | collective-permute-start | bytes 2359304 | tf_op jit(solution)/shard_map/ppermute | solution.py:1042
  336.4 11.2 %copy-start.9 = (f32[2,48,384]{2,1,0:T(8,128)S(1)}, f32[2,48,384]{2,1,0:T(8,128)}, u32[]{:S(2)}) copy-start(f32[2,48,384]{2,1,0:T(8,128)} %get-tuple-element.140) | copy-start | bytes 442372
  345.6 2.7 copy-start.10
  345.6 3.3 copy-start.7
  345.6 4.0 %copy-start.6 = (f32[1,48,1536]{2,1,0:T(8,128)S(1)}, f32[1,48,1536]{2,1,0:T(8,128)}, u32[]{:S(2)}) copy-start(f32[1,48,1536]{2,1,0:T(8,128)} %get-tuple-element.98) | copy-start | bytes 884740
where the time goes:
time: 351 us; the launch traced here: 350 us
  Pallas kernels  275 us (78%)
  other arithmetic  19.7 us (6%)
  matrix products  19.3 us (5%)
  local copies, waits for them, and re-layouts  13.7 us (4%)
  starting transfers between devices  11.9 us (3%)
  waiting for transfers between devices  9.42 us (3%)
    pallas_call x1, Pallas kernels, scatter_gradients(): pl.pallas_call(functools.partial(scatter_kernel, subs, count), out_shape=...  96 us
    pallas_call x1, Pallas kernels, gather_weights(): pl.pallas_call(functools.partial(gather_kernel, subs, count, wholes), out...  63 us
    pallas_call x1, Pallas kernels, attention_forward(): pl.pallas_call(functools.partial(forward_kernel, subs), grid=(pairs,), ou...  57.1 us
    pallas_call x1, Pallas kernels, ffn_forward(): pl.pallas_call(functools.partial(ffn_forward_kernel, subs), grid=(units /...  22 us
    pallas_call x1, Pallas kernels, ffn_backward(): pl.pallas_call(ffn_backward_kernel, grid=(units // BLOCK,), out_shape=[ja...  20.8 us
    pallas_call x1, Pallas kernels, attention_backward(): pl.pallas_call(backward_kernel, grid=(pairs,), out_shape=[jax.ShapeDtypeS...  16 us
  transfers between devices with their start and end apart: 4, of which 2 were waited for; matrix products, arithmetic and copies ran while one was open for 8% of the time, Pallas kernels for 0%

commit v1 on v0

--- a/solution.py
+++ b/solution.py
@@ -72,6 +72,7 @@
         self.sub = rank % subs
         block = rank // subs
         self.z = block // 4
+        self.turns = [(self.z + step) % 4 for step in range(4)]
         self.x = (block // 2) % 2
         self.c = block % 2
         self.y = lax.axis_index("tensor")
@@ -347,25 +348,60 @@
     return full.reshape(full.shape[0], GRID * full.shape[4], full.shape[5])
 
 
+class Last:
+    def __init__(self, place, piece, total, from_z, send, recv):
+        self.place, self.piece, self.total, self.from_z = place, piece, total, from_z
+        self.send, self.recv = send, recv
+
+    def start(self):
+        p = self.place
+        for step in (1, 2, 3):
+            remote(
+                self.piece.at[:, p.turns[step]],
+                self.from_z.at[step - 1],
+                self.send.at[step - 1],
+                self.recv.at[step - 1],
+                p.z_peer(step),
+            ).start()
+
+    def finish(self):
+        p = self.place
+        for step in (0, 1, 2):
+            slot = self.from_z.at[step]
+            remote(slot, slot, self.send.at[step], self.recv.at[step], p.sibling()).wait()
+
+        def step(i, carry):
+            total = self.piece[i, p.z].astype(F32)
+            for s in range(3):
+                total = total + self.from_z[s, i].astype(F32)
+            self.total[i] = total
+            return carry
+
+        lax.fori_loop(0, self.total.shape[0], step, 0)
+
+
 class Scatter:
-    def __init__(self, place, part, total, mine, from_core, from_second, from_first, from_z, send, recv, local):
-        self.place, self.part, self.total = place, part, total
+    def __init__(self, place, part, mine, from_core, from_second, from_first, send, recv, local):
+        self.place, self.part = place, part
         self.mine, self.from_core = mine, from_core
-        self.from_second, self.from_first, self.from_z = from_second, from_first, from_z
+        self.from_second, self.from_first = from_second, from_first
         self.send, self.recv, self.local = send, recv, local
-        self.m, self.rows, self.w = total.shape
-        self.started = []
+        self.m, _, self.rows, self.w = from_first.shape
 
     def cols(self, y):
         return pl.ds(pl.multiple_of(y * self.w, LANES), self.w)
 
     def copy(self, index, src, dst, peer):
-        step = remote(src, dst, self.send.at[index], self.recv.at[index], peer)
-        step.start()
-        self.started.append(step)
+        remote(src, dst, self.send.at[index], self.recv.at[index], peer).start()
 
     def arrive(self, index, ref):
         remote(ref, ref, self.send.at[index], self.recv.at[index], self.place.sibling()).wait_recv()
+
+    def drain(self):
+        for index in range(7):
+            remote(
+                self.from_first, self.from_first, self.send.at[index], self.recv.at[index], self.place.sibling()
+            ).wait_send()
 
     def add(self, target, source):
         m = self.m
@@ -377,17 +413,16 @@
 
         lax.fori_loop(0, m * 4, step, 0)
 
+    def keep(self, slot, spot):
+        x, y = self.place.pieces()[spot]
+        source = self.part.at[:, :, x, self.place.c, :, self.cols(y)]
+        return pltpu.make_async_copy(source, self.mine.at[slot], self.local.at[slot])
+
     def stage1(self):
         p = self.place
         spots = p.pieces()
-        self.kept = []
         for slot, (here, there) in enumerate(((3, 3), (2, 1), (1, 2), (0, 0))):
-            x, y = spots[here]
-            keep = pltpu.make_async_copy(
-                self.part.at[:, :, x, p.c, :, self.cols(y)], self.mine.at[slot], self.local.at[slot]
-            )
-            keep.start()
-            self.kept.append(keep)
+            self.keep(slot, here).start()
             x, y = spots[there]
             self.copy(
                 slot,
@@ -397,7 +432,7 @@
             )
 
     def joined(self, slot):
-        self.kept[slot].wait()
+        self.keep(slot, 3 - slot).wait()
         self.arrive(slot, self.from_core.at[slot])
         self.add(self.mine.at[slot], self.from_core.at[slot])
 
@@ -418,32 +453,8 @@
         self.add(self.mine.at[3], self.from_second.at[1])
 
     def stage4(self):
-        p = self.place
         self.arrive(6, self.from_first)
         self.add(self.mine.at[3], self.from_first)
-        for step in (1, 2, 3):
-            self.copy(
-                6 + step, self.mine.at[3, :, (p.z + step) % 4], self.from_z.at[step - 1], p.z_peer(step)
-            )
-
-    def stage5(self):
-        p = self.place
-        for step in (1, 2, 3):
-            self.arrive(6 + step, self.from_z.at[step - 1])
-
-        def step(i, carry):
-            total = self.mine[3, i, p.z].astype(F32)
-            for s in range(3):
-                total = total + self.from_z[s, i].astype(F32)
-            self.total[i] = total
-            return carry
-
-        lax.fori_loop(0, self.m, step, 0)
-        for step in self.started:
-            step.wait_send()
-
-    def stages(self):
-        return [self.stage1, self.stage2, self.stage3, self.stage4, self.stage5]
 
 
 class Sum:
@@ -485,46 +496,74 @@
         pltpu.VMEM((4, m, 4, rows, w), BF16),
         pltpu.VMEM((2, m, 4, rows, w), BF16),
         pltpu.VMEM((m, 4, rows, w), BF16),
-        pltpu.VMEM((3, m, rows, w), BF16),
-        pltpu.SemaphoreType.DMA((10,)),
-        pltpu.SemaphoreType.DMA((10,)),
+        pltpu.SemaphoreType.DMA((7,)),
+        pltpu.SemaphoreType.DMA((7,)),
         pltpu.SemaphoreType.DMA((4,)),
     ]
 
 
-def scatter_kernel(subs, count, *refs):
-    parts, small = refs[:count], refs[count]
-    totals, small_total = refs[count + 1 : 2 * count + 1], refs[2 * count + 1]
-    scratch = refs[2 * count + 2 :]
+def last_scratch(shape):
+    return [
+        pltpu.VMEM((3,) + shape, BF16),
+        pltpu.SemaphoreType.DMA((3,)),
+        pltpu.SemaphoreType.DMA((3,)),
+    ]
+
+
+def as_shards(part):
+    m, rows, w = part.shape
+    return part.reshape(m, 4, 2, 2, rows // GRID, w)
+
+
+def scatter_kernel(subs, early, count, *refs):
+    pieces, parts, small = refs[:early], refs[early : early + count], refs[early + count]
+    refs = refs[early + count + 1 :]
+    totals, small_total = refs[: early + count], refs[early + count]
+    refs = refs[early + count + 1 :]
+    lasts, refs = refs[: 3 * (early + count)], refs[3 * (early + count) :]
     place = Place(subs)
     entry_barrier(place)
-    movers = [
-        Scatter(place, parts[i], totals[i], *scratch[8 * i : 8 * i + 8]) for i in range(count)
-    ]
-    running, box, send, recv = scratch[8 * count :]
+    movers = [Scatter(place, parts[i], *refs[7 * i : 7 * i + 7]) for i in range(count)]
+    sources = list(pieces) + [mover.mine.at[3] for mover in movers]
+    ends = [Last(place, sources[i], totals[i], *lasts[3 * i : 3 * i + 3]) for i in range(early + count)]
+    running, box, send, recv = refs[7 * count :]
     small_sum = Sum(place, small, running, box, send, recv)
     for mover in movers:
         mover.stage1()
-    steps = [s for s in wavefront(movers) if s.__func__ is not Scatter.stage1]
+    for end in ends[:early]:
+        end.start()
     extra = small_sum.stages()
+    steps = []
+    for time in range(count + 4):
+        for index in range(count):
+            stage = time - index
+            if 0 <= stage < 5:
+                mover, end = movers[index], ends[early + index]
+                steps.append((mover.stage2, mover.stage3, mover.stage4, end.start, end.finish)[stage])
     for index, step in enumerate(steps):
         if index < len(extra):
             extra[index]()
         step()
     for step in extra[len(steps) :]:
         step()
+    for end in ends[:early]:
+        end.finish()
+    for mover in movers:
+        mover.drain()
     small_total[...] = running[4]
 
 
-def scatter_gradients(subs, parts, small):
-    count = len(parts)
-    rows = parts[0].shape[1] // GRID
-    shaped = [p.reshape(p.shape[0], 4, 2, 2, rows, p.shape[2]) for p in parts]
-    shapes = [(p.shape[0], rows, p.shape[2] // 2) for p in parts]
-    outs = [jax.ShapeDtypeStruct(s, F32) for s in shapes]
+def scatter_gradients(subs, pieces, parts, small):
+    early, count = len(pieces), len(parts)
+    shaped = [as_shards(p) for p in parts]
+    shapes = [(p.shape[0],) + p.shape[2:] for p in pieces]
+    whole = [(p.shape[0], p.shape[4], p.shape[5] // 2) for p in shaped]
+    outs = [jax.ShapeDtypeStruct(s, F32) for s in shapes + whole]
     outs.append(jax.ShapeDtypeStruct(small.shape, F32))
     scratch = []
-    for s in shapes:
+    for s in shapes + whole:
+        scratch += last_scratch(s)
+    for s in whole:
         scratch += scatter_scratch(s)
     scratch += [
         pltpu.VMEM((5,) + small.shape, F32),
@@ -532,18 +571,19 @@
         pltpu.SemaphoreType.DMA((5,)),
         pltpu.SemaphoreType.DMA((5,)),
     ]
+    local = pl.BlockSpec(memory_space=pltpu.VMEM)
     results = pl.pallas_call(
-        functools.partial(scatter_kernel, subs, count),
+        functools.partial(scatter_kernel, subs, early, count),
         out_shape=outs,
-        in_specs=[pl.BlockSpec(memory_space=pl.ANY)] * count + [pl.BlockSpec(memory_space=pltpu.VMEM)],
-        out_specs=[pl.BlockSpec(memory_space=pltpu.VMEM)] * (count + 1),
+        in_specs=[local] * early + [pl.BlockSpec(memory_space=pl.ANY)] * count + [local],
+        out_specs=[local] * (early + count + 1),
         scratch_shapes=scratch,
         compiler_params=pltpu.CompilerParams(
             collective_id=1, has_side_effects=True, vmem_limit_bytes=VMEM_LIMIT
         ),
         name="scatter_gradients",
-    )(*shaped, small)
-    return results[:count], results[count]
+    )(*pieces, *shaped, small)
+    return results[:-1], results[-1]
 
 
 def head_lanes(half):
@@ -688,70 +728,188 @@
     )(both, wq, wkv, biases, facts, up, down)
 
 
-def backward_kernel(probs, qw, qe, keys, values, ctx, dctx, ent_col, ent_row, dqw, dqe, dkeys, dvalues):
-    queries = jnp.concatenate([qw[...], qe[...]], axis=1)
-    value = values[...]
-    turned = keys[...].T
-    ent = ent_col[...] == 1
-    ent_lane = ent_row[...] == 1
-    grad = dctx[...]
-    zero = jnp.zeros_like(value)
-    dk, dv = [], []
-    for half in range(2):
-        lanes = head_lanes(half)
-        here = slice(half * HEAD, (half + 1) * HEAD)
-        prob = probs[half]
-        delta = jnp.sum(
-            ctx[here, :].astype(F32) * grad[here, :].astype(F32), axis=0, keepdims=True
-        )
-        dprob = dot_nn(jnp.where(lanes, value, zero), grad)
-        dscore = (prob.astype(F32) * (dprob - delta)).astype(BF16)
-        key_t = turned[here, :]
-        none = jnp.zeros_like(key_t)
-        tall = jnp.concatenate(
-            [jnp.where(ent_lane, none, key_t), jnp.where(ent_lane, key_t, none)], axis=0
-        )
-        dq = dot_nn(tall, dscore) * (HEAD ** (-0.5))
-        dqw[here, :] = dq[:HEAD].astype(BF16)
-        dqe[here, :] = dq[HEAD:].astype(BF16)
-        both = dot_nn(dscore, queries)
-        dk.append(jnp.where(ent, both[:, LANES:], both[:, :LANES]))
-        dv.append(dot_nt(prob, grad))
-    dkeys[...] = jnp.where(head_lanes(0), dk[0], dk[1]).astype(BF16)
-    dvalues[...] = jnp.where(head_lanes(0), dv[0], dv[1]).astype(BF16)
-
-
-def attention_backward(probs, qw, qe, keys, values, ctx, dctx, ent_col, ent_row):
-    rows, width = qw.shape
-    length = keys.shape[0]
+def backward_kernel(
+    subs, both, facts, probs, word, entity, keys, values, ctx, dctx, wq, wkv, d_one, down_part, up_part,
+    q_part, kv_part, input_grad, q_bias, v_bias, down_piece, up_piece,
+    column, turned_rows, pair_grad, pair_got, pair_send, pair_recv, *scratch,
+):
+    place = Place(subs)
+    step = pl.program_id(0)
+    pairs = pl.num_programs(0) - 1
+    rows = word.shape[0]
+    movers = [Scatter(place, down_part, *scratch[:7]), Scatter(place, up_part, *scratch[7:])]
+    own = pl.ds(pl.multiple_of(place.c * rows, LANES), rows)
+    other = pl.ds(pl.multiple_of((1 - place.c) * rows, LANES), rows)
+
+    @pl.when(step == 0)
+    def _():
+        entry_barrier(place)
+        for mover in movers:
+            mover.stage1()
+        column[...] = facts[place.y].T
+        turned_rows[...] = both[place.c].T
+        input_grad[...] = d_one[...]
+
+    @pl.when(step == 1)
+    def _():
+        movers[0].stage2()
+
+    @pl.when(step == 2)
+    def _():
+        movers[1].stage2()
+
+    @pl.when(step == 5)
+    def _():
+        movers[0].stage3()
+
+    @pl.when(step < pairs)
+    def _():
+        queries = jnp.concatenate([word[...], entity[...]], axis=1)
+        value = values[...]
+        turned = keys[...].T
+        ent = column[:, 1:2] == 1
+        ent_lane = facts[place.y, 1:2, :] == 1
+        own_ent = facts[place.y, 1:2, own] == 1
+        grad = dctx[...]
+        zero = jnp.zeros_like(value)
+        dk, dv, dw, de = [], [], [], []
+        for half in range(2):
+            lanes = head_lanes(half)
+            here = slice(half * HEAD, (half + 1) * HEAD)
+            prob = probs[half]
+            delta = jnp.sum(
+                ctx[here, :].astype(F32) * grad[here, :].astype(F32), axis=0, keepdims=True
+            )
+            dprob = dot_nn(jnp.where(lanes, value, zero), grad)
+            dscore = (prob.astype(F32) * (dprob - delta)).astype(BF16)
+            key_t = turned[here, :]
+            none = jnp.zeros_like(key_t)
+            tall = jnp.concatenate(
+                [jnp.where(ent_lane, none, key_t), jnp.where(ent_lane, key_t, none)], axis=0
+            )
+            dq = dot_nn(tall, dscore) * (HEAD ** (-0.5))
+            dw.append(dq[:HEAD])
+            de.append(dq[HEAD:])
+            pair = dot_nn(dscore, queries)
+            dk.append(jnp.where(ent, pair[:, LANES:], pair[:, :LANES]))
+            dv.append(dot_nt(prob, grad))
+        first = head_lanes(0)
+        pair_grad[step, :, :LANES] = jnp.where(first, dk[0], dk[1]).astype(BF16)
+        pair_grad[step, :, LANES:] = jnp.where(first, dv[0], dv[1]).astype(BF16)
+        remote(
+            pair_grad.at[step, other], pair_got.at[step], pair_send.at[step], pair_recv.at[step], place.sibling()
+        ).start()
+        d_word, d_ent = jnp.concatenate(dw, axis=0), jnp.concatenate(de, axis=0)
+        empty = jnp.zeros_like(d_word)
+        turned_grad = jnp.concatenate(
+            [
+                jnp.where(own_ent, empty, d_word),
+                jnp.where(own_ent, empty, d_ent),
+                jnp.where(own_ent, d_word, empty),
+                jnp.where(own_ent, d_ent, empty),
+            ],
+            axis=0,
+        ).astype(BF16)
+        query_grad = turned_grad.T
+        weights = jnp.concatenate([wq[m] for m in range(4)], axis=1)
+        input_grad[...] += dot_nt(query_grad, weights)
+        part = dot_nn(turned_rows[...], query_grad).astype(BF16)
+        sums = column_sum(query_grad.astype(F32))
+        for m in range(4):
+            span = slice(m * LANES, (m + 1) * LANES)
+            q_part[m] = part[:, span]
+            q_bias[m : m + 1] = sums[:, span]
+
+    @pl.when(step > 0)
+    def _():
+        before = step - 1
+        remote(
+            pair_got.at[before], pair_got.at[before], pair_send.at[before], pair_recv.at[before], place.sibling()
+        ).wait()
+        grad = (pair_grad[before, own].astype(F32) + pair_got[before].astype(F32)).astype(BF16)
+        weights = jnp.concatenate([wkv[0], wkv[1]], axis=1)
+        input_grad[...] += dot_nt(grad, weights)
+        part = dot_nn(turned_rows[...], grad).astype(BF16)
+        kv_part[0] = part[:, :LANES]
+        kv_part[1] = part[:, LANES:]
+        v_bias[0:1] = column_sum(grad[:, LANES:].astype(F32))
+
+    @pl.when(step == pairs)
+    def _():
+        movers[1].stage3()
+        for mover in movers:
+            mover.stage4()
+            mover.drain()
+        down_piece[...] = movers[0].mine[3]
+        up_piece[...] = movers[1].mine[3]
+
+
+def attention_backward(subs, both, facts, probs, word, entity, keys, values, ctx, dctx, wq, wkv, d_one, down_part, up_part):
+    _, rows, width = both.shape
+    length = 2 * rows
     pairs = width // LANES
-    block = lambda n: pl.BlockSpec((n, LANES), lambda i: (0, i))
-    turned = pl.BlockSpec((LANES, rows), lambda i: (i, 0))
-    whole = lambda a: pl.BlockSpec(a.shape, lambda i: (0,) * a.ndim)
+    block = lambda n: pl.BlockSpec((n, LANES), lambda i: (0, jnp.minimum(i, pairs - 1)))
+    behind = lambda n: pl.BlockSpec((n, LANES), lambda i: (0, jnp.maximum(i - 1, 0)))
+    turned = pl.BlockSpec((LANES, rows), lambda i: (jnp.minimum(i, pairs - 1), 0))
+    whole = lambda a: pl.BlockSpec(a.shape, lambda i: (0,) * a.ndim, pipeline_mode=pl.Buffered(1))
+    q_cols = pl.BlockSpec((4, width, LANES), lambda i: (0, 0, jnp.minimum(i, pairs - 1)))
+    kv_cols = pl.BlockSpec((2, width, LANES), lambda i: (0, 0, jnp.maximum(i - 1, 0)))
+    anywhere = pl.BlockSpec(memory_space=pl.ANY)
+    local = pl.BlockSpec(memory_space=pltpu.VMEM)
+    shape = (1, down_part.shape[1] // GRID, down_part.shape[2] // 2)
+    piece = jax.ShapeDtypeStruct((1, 4) + shape[1:], BF16)
     return pl.pallas_call(
-        backward_kernel,
-        grid=(pairs,),
+        functools.partial(backward_kernel, subs),
+        grid=(pairs + 1,),
         out_shape=[
-            jax.ShapeDtypeStruct((width, rows), BF16),
-            jax.ShapeDtypeStruct((width, rows), BF16),
-            jax.ShapeDtypeStruct((length, width), BF16),
-            jax.ShapeDtypeStruct((length, width), BF16),
+            jax.ShapeDtypeStruct(wq.shape, BF16),
+            jax.ShapeDtypeStruct(wkv.shape, BF16),
+            jax.ShapeDtypeStruct((rows, width), F32),
+            jax.ShapeDtypeStruct((8, width), F32),
+            jax.ShapeDtypeStruct((8, width), F32),
+            piece,
+            piece,
         ],
         in_specs=[
-            pl.BlockSpec((2, length, rows), lambda i: (i, 0, 0)),
+            whole(both),
+            whole(facts),
+            pl.BlockSpec((2, length, rows), lambda i: (jnp.minimum(i, pairs - 1), 0, 0)),
             block(rows),
             block(rows),
             block(length),
             block(length),
             turned,
             turned,
-            whole(ent_col),
-            whole(ent_row),
+            q_cols,
+            kv_cols,
+            whole(d_one),
+            anywhere,
+            anywhere,
         ],
-        out_specs=[turned, turned, block(length), block(length)],
-        compiler_params=pltpu.CompilerParams(vmem_limit_bytes=VMEM_LIMIT),
+        out_specs=[
+            q_cols,
+            kv_cols,
+            pl.BlockSpec((rows, width), lambda i: (0, 0), pipeline_mode=pl.Buffered(1)),
+            block(8),
+            behind(8),
+            local,
+            local,
+        ],
+        scratch_shapes=[
+            pltpu.VMEM((length, facts.shape[1]), jnp.int32),
+            pltpu.VMEM((width, rows), BF16),
+            pltpu.VMEM((pairs, length, 2 * LANES), BF16),
+            pltpu.VMEM((pairs, rows, 2 * LANES), BF16),
+            pltpu.SemaphoreType.DMA((pairs,)),
+            pltpu.SemaphoreType.DMA((pairs,)),
+        ]
+        + scatter_scratch(shape)
+        + scatter_scratch(shape),
+        compiler_params=pltpu.CompilerParams(
+            collective_id=3, has_side_effects=True, vmem_limit_bytes=VMEM_LIMIT
+        ),
         name="attention_backward",
-    )(probs, qw, qe, keys, values, ctx, dctx, ent_col, ent_row)
+    )(both, facts, probs, word, entity, keys, values, ctx, dctx, wq, wkv, d_one, as_shards(down_part), as_shards(up_part))
 
 
 def ffn_forward_kernel(
@@ -953,10 +1111,6 @@
         other = d + subs if (d // subs) % 2 == 0 else d - subs
         y = 1 - (d // subs) % 2
         trades.append((d * pairs + y, other * pairs + 1 - y))
-    siblings = [
-        (d, d + subs if (d // subs) % 2 == 0 else d - subs) for d in range(lax.axis_size("dp"))
-    ]
-
     def trade(own):
         got = lax.ppermute(own, ("dp", "tensor"), trades)
         return jnp.where(moved, got, own)
@@ -990,14 +1144,8 @@
     w_up, w_down_t = as_matrix(w_up)[0], as_matrix(w_down_t)[0]
     ffn_bias_full = biases[:, 5:used].reshape(units)
     facts = lax.dynamic_index_in_dim(pair_facts, rank, 0, keepdims=False)
-    segment, entity, valid_mask = facts[0], facts[1], facts[2]
-    layer_input = lax.dynamic_index_in_dim(both, core, 0, keepdims=False)
-
-    ent_own = lax.dynamic_slice_in_dim(entity, start, rows)
-    valid_own = lax.dynamic_slice_in_dim(valid_mask, start, rows).astype(F32)[:, None]
-    ent_col = entity[:, None]
-    ent_row = entity[None, :]
-
+
+    valid_own = lax.dynamic_slice_in_dim(facts[2], start, rows).astype(F32)[:, None]
     grad_out, context_t = lax.optimization_barrier((grad_out, context_t))
     active, slope, hidden_low, normal_one, inverse_one, result, d_two, sums_two = ffn_forward(
         subs, both, context_t, w_out_t, w_up, w_down_t, ffn_bias_full[None], out_bias, ln_gain, ln_bias, valid_own,
@@ -1008,45 +1156,18 @@
         d_two, hidden_low, active, slope, w_up, w_down_t, context_t, w_out_t, ln_gain, normal_one, inverse_one
     )
 
-    d_word_t, d_ent_t, d_keys_all, d_values_all = attention_backward(
-        probs, query_word, query_ent, keys, values, context_t, d_context_t, ent_col, ent_row
-    )
-    stacked = jnp.stack([d_keys_all, d_values_all]).reshape(2, 2, rows, width)
-    mine = lax.dynamic_index_in_dim(stacked, core, 1, keepdims=False)
-    theirs = lax.dynamic_index_in_dim(stacked, 1 - core, 1, keepdims=False)
-    swapped = lax.ppermute(theirs, "dp", siblings)
-    d_kv = (mine.astype(F32) + swapped.astype(F32)).astype(BF16)
-
-    ent_lane = (ent_own == 1)[None, :]
-    none = jnp.zeros_like(d_word_t)
-    d_queries_t = jnp.stack(
-        [
-            jnp.where(ent_lane, none, d_word_t),
-            jnp.where(ent_lane, none, d_ent_t),
-            jnp.where(ent_lane, d_word_t, none),
-            jnp.where(ent_lane, d_ent_t, none),
-        ]
-    )
-    query_part = jnp.einsum(
-        "ld,mel->mde", layer_input, d_queries_t, preferred_element_type=F32
-    ).astype(BF16)
-    kv_part = jnp.einsum("ld,mle->mde", layer_input, d_kv, preferred_element_type=F32).astype(BF16)
-    attn_bias_part = jnp.concatenate(
-        [jnp.sum(d_queries_t.astype(F32), 2), jnp.sum(d_kv[1].astype(F32), 0)[None]], 0
-    )
-    input_grad = (
-        d_one
-        + jnp.einsum("mel,mde->ld", d_queries_t, w_q, preferred_element_type=F32)
-        + jnp.einsum("mle,mde->ld", d_kv, w_kv, preferred_element_type=F32)
+    query_part, kv_part, input_grad, q_bias, v_bias, down_piece, up_piece = attention_backward(
+        subs, both, pair_facts, probs, query_word, query_ent, keys, values, context_t, d_context_t, w_q, w_kv, d_one,
+        down_part[None], up_part[None],
     )
     returned = lax.ppermute(input_grad.astype(BF16), ("dp", "tensor"), trades)
     input_grad = jnp.where(moved, returned.astype(F32), input_grad)
 
-    small = jnp.concatenate([sums_one.reshape(-1), sums_two.reshape(-1), attn_bias_part.reshape(-1), ffn_bias_part[0]])
+    small = jnp.concatenate([sums_one.reshape(-1), sums_two.reshape(-1), q_bias[:4].reshape(-1), v_bias[0], ffn_bias_part[0]])
     padded = -(-small.shape[0] // (8 * LANES)) * 8 * LANES
     small = jnp.pad(small, (0, padded - small.shape[0])).reshape(-1, LANES)
     sums, small_sum = scatter_gradients(
-        subs, [down_part[None], up_part[None], out_part[None], query_part, kv_part], small
+        subs, [down_piece, up_piece], [out_part[None], query_part, kv_part], small
     )
     if subs > 1:
         sums = [

time: 351 us -> 333 us (0.949)
  matrix products: 19.3 us -> 0 us
  other arithmetic: 19.7 us -> 11.5 us
  waiting for transfers between devices: 9.42 us -> 16.9 us
  Pallas kernels: 275 us -> 281 us
  starting transfers between devices: 11.9 us -> 8.16 us
    dot_general x4 -> x0, matrix products: 19.3 us -> none  [the longest x1 6.31 us: body(): jnp.einsum('ld,mel->mde', layer_input, d_queries_t, preferred_element_typ...]
    pallas_call x2, Pallas kernels: 112 us -> 118 us  [the longest x1 65.1 us: scatter_gradients(): pl.pallas_call(functools.partial(scatter_kernel, subs, early, count), out...]
    ppermute x2, waiting for transfers between devices: 4.58 us -> 9.32 us  [trade(): got = lax.ppermute(own, ('dp', 'tensor'), trades)]
  transfers between devices with their start and end apart: 4 -> 3, of which waited for: 2 -> 3; matrix products, arithmetic and copies ran while one was open for 8% -> 3% of each run, Pallas kernels for 0% -> 0%
where the time goes in v1:
time: 333 us; the launch traced here: 332 us
  Pallas kernels  281 us (84%)
  waiting for transfers between devices  16.9 us (5%)
  local copies, waits for them, and re-layouts  12.7 us (4%)
  other arithmetic  11.5 us (3%)
  starting transfers between devices  8.16 us (2%)
    pallas_call x1, Pallas kernels, scatter_gradients(): pl.pallas_call(functools.partial(scatter_kernel, subs, early, count), out...  65.1 us
    pallas_call x1, Pallas kernels, gather_weights(): pl.pallas_call(functools.partial(gather_kernel, subs, count, wholes), out...  63 us
    pallas_call x1, Pallas kernels, attention_forward(): pl.pallas_call(functools.partial(forward_kernel, subs), grid=(pairs,), ou...  57.2 us
    pallas_call x1, Pallas kernels, attention_backward(): pl.pallas_call(functools.partial(backward_kernel, subs), grid=(pairs + 1,...  53 us
    pallas_call x1, Pallas kernels, ffn_forward(): pl.pallas_call(functools.partial(ffn_forward_kernel, subs), grid=(units /...  21.8 us
    pallas_call x1, Pallas kernels, ffn_backward(): pl.pallas_call(ffn_backward_kernel, grid=(units // BLOCK,), out_shape=[ja...  20.7 us
    ppermute x2, waiting for transfers between devices, trade(): got = lax.ppermute(own, ('dp', 'tensor'), trades)  9.32 us
    ppermute x1, waiting for transfers between devices, body(): returned = lax.ppermute(input_grad.astype(BF16), ('dp', 'tensor'), trades)  7.55 us
  transfers between devices with their start and end apart: 3, of which 3 were waited for; matrix products, arithmetic and copies ran while one was open for 3% of the time, Pallas kernels for 0%

profile of v1, /device:TPU:1, one launch (start us, length us, event | category | flops | bytes accessed | tf_op | source)
XLA Modules:
  0.0 331.7 jit_solution(11251389898214882953)
XLA Ops:
  0.6 0.7 reshape.89
  1.3 1.3 fusion.3.refs_6_
  2.7 0.7 pad_add_fusion
  3.4 0.6 pad.16.refs_7_
  4.0 63.0 %gather_weights.1 = (bf16[2,4,2,2,48,768]{5,4,3,2,1,0:T(8,128)(2,1)}, bf16[4,4,2,2,48,768]{5,4,3,2,1,0:T(8,128)(2,1)}, bf16[1,4,2,2,48,768]{5,4,3,2,1,0:T(8,128)...) custom-call(bf16[2,48,384]{2,1,0:T(8,128)(2,1)} %refs_0_.1, ...), custom_call_target="tpu_custom_call" | custom-call | tf_op jit(solution)/shard_map/gather_weights/pallas_call | solution.py:327
  67.0 0.0 copy-start.1
  67.0 57.2 %attention_forward.1 = (bf16[768,512]{1,0:T(8,128)(2,1)}, bf16[12,1024,512]{2,1,0:T(8,128)(2,1)}, bf16[512,768]{1,0:T(8,128)(2,1)}, bf16[512,768]{1,0:T(8,128)(2...) custom-call(bf16[2,512,768]{2,1,0:T(8,128)(2,1)} %get-tuple-element., ...), custom_call_target="tpu_custom_call", output_to_operand_aliasing={{6}: (5, {}), {7}: (6, {})} | custom-call | tf_op jit(solution)/shard_map/attention_forward/pallas_call | solution.py:685
  124.3 0.0 copy-done.1
  124.3 2.6 collective-permute-start
  126.9 0.8 slice.77
  127.7 0.6 broadcast_in_dim_reshape.3.unit_bias
  128.3 0.8 fusion.4
  129.1 0.9 copy.30.valid
  130.0 7.6 %collective-permute-done = bf16[512,768]{1,0:T(8,128)(2,1)S(1)} collective-permute-done((bf16[512,768]{1,0:T(8,128)(2,1)S(1)}, bf16[512,768]{1,0:T(8,128)(2,1)S(1)}, u32[]{:S(2)}, u32[]{:S(2)}) %collective-permute-start) | collective-permute-done | bytes 786464 | tf_op jit(solution)/shard_map/ppermute | solution.py:1115
  137.6 1.0 broadcast_select_fusion.1.grad_out
  138.5 21.8 %ffn_forward.1 = (bf16[512,3072]{1,0:T(8,128)(2,1)}, bf16[512,3072]{1,0:T(8,128)(2,1)}, bf16[512,768]{1,0:T(8,128)(2,1)}, f32[512,768]{1,0:T(8,128)}, f32[512,1]...) custom-call(bf16[2,512,768]{2,1,0:T(8,128)(2,1)} %get-tuple-element.59.both, ...), custom_call_target="tpu_custom_call" | custom-call | flops 5435817984 | bytes 16908288 | tf_op jit(solution)/shard_map/ffn_forward/pallas_call | solution.py:968
  160.4 0.0 copy-start.9
  160.4 20.7 %ffn_backward.1 = (bf16[768,3072]{1,0:T(8,128)(2,1)}, bf16[768,3072]{1,0:T(8,128)(2,1)}, f32[1,3072]{1,0:T(1,128)}, f32[512,768]{1,0:T(8,128)}, bf16[768,512]{1,...) custom-call(f32[512,768]{1,0:T(8,128)} %get-tuple-element.78.d_two, ...), custom_call_target="tpu_custom_call" | custom-call | flops 10871635968 | bytes 28704768 | tf_op jit(solution)/shard_map/ffn_backward/pallas_call | solution.py:1045
  181.1 0.7 reshape.94
  181.9 0.0 copy-start.10
  181.9 53.0 %attention_backward.1 = (bf16[4,768,768]{2,1,0:T(8,128)(2,1)}, bf16[2,768,768]{2,1,0:T(8,128)(2,1)}, f32[512,768]{1,0:T(8,128)}, f32[8,768]{1,0:T(8,128)}, f32[8...) custom-call(bf16[2,512,768]{2,1,0:T(8,128)(2,1)} %get-tuple-element.59.both, ...), custom_call_target="tpu_custom_call" | custom-call | tf_op jit(solution)/shard_map/attention_backward/pallas_call | solution.py:861
  234.9 0.7 slice.79
  235.7 0.8 slice_reduce_fusion.1
  236.5 0.6 pad_bitcast_fusion.refs_5_
  237.1 65.1 %scatter_gradients.1 = (f32[1,48,1536]{2,1,0:T(8,128)}, f32[1,48,1536]{2,1,0:T(8,128)}, f32[1,48,384]{2,1,0:T(8,128)}, f32[4,48,384]{2,1,0:T(8,128)}, f32[2,48,384]{2,1,0:T(8,128)}, /*index=5*/f32[152,128]{1,0:T(8,128)}) custom-call(bf16[1,4,48,1536]{3,2,1,0:T(8,128)(2,1)} %get-tuple-element.89.refs_0_, bf16[1,4,48,1536]{3,2,1,0:T(8,128)(2,1)} %get-tuple-element.90.refs_1_, ...), custom_call_target="tpu_custom_call" | custom-call | tf_op jit(solution)/shard_map/scatter_gradients/pallas_call | solution.py:575
  302.3 0.9 slice_bitcast_fusion
  303.2 0.8 slice_bitcast_fusion.2
  304.0 1.9 collective-permute-start.1
  305.9 1.0 convert_element_type.26
  306.9 3.6 %collective-permute-start.2 = (bf16[512,768]{1,0:T(8,128)(2,1)}, bf16[512,768]{1,0:T(8,128)(2,1)}, u32[]{:S(2)}, u32[]{:S(2)}) collective-permute-start(bf16[512,768]{1,0:T(8,128)(2,1)} %convert_element_type.26), channel_id=1, source_target_pairs={{1,2},{2,1},{5,6},{6,5},{9,10},{10,9},{13,14},{14,13},{17,18},{18,... | collective-permute-start | bytes 2359304 | tf_op jit(solution)/shard_map/ppermute | solution.py:1163
  310.5 0.6 pad_maximum_fusion
  311.1 0.6 pad_maximum_fusion.1
  311.8 0.1 reduce_sum.14
  311.9 0.5 slice.99
  312.4 0.1 reduce_sum.18
  313.1 0.7 dynamic_slice.16
  313.8 0.6 pad_maximum_fusion.2
  314.4 0.6 constant_dynamic-slice_fusion
  315.0 0.5 divide_sqrt_fusion
  315.6 1.7 collective-permute-done.1
  317.3 1.0 broadcast_select_fusion
  318.3 7.5 %collective-permute-done.2 = bf16[512,768]{1,0:T(8,128)(2,1)} collective-permute-done((bf16[512,768]{1,0:T(8,128)(2,1)}, bf16[512,768]{1,0:T(8,128)(2,1)}, u32[]{:S(2)}, u32[]{:S(2)}) %collective-permute-start.2) | collective-permute-done | bytes 786464 | tf_op jit(solution)/shard_map/ppermute | solution.py:1163
  325.8 2.4 convert_select_fusion
  328.2 0.7 copy.54
  328.9 0.7 copy.55
  329.6 0.6 copy.56
  330.2 0.7 copy.57
  331.0 0.7 copy.58
  (32 shorter events, 0.1 us)
Async XLA Ops:
  67.0 57.3 %copy-start.1 = (bf16[512,768]{1,0:T(8,128)(2,1)S(1)}, bf16[512,768]{1,0:T(8,128)(2,1)}, u32[]{:S(2)}) copy-start(bf16[512,768]{1,0:T(8,128)(2,1)} %param.16) | copy-start | bytes 2359300
  124.3 13.3 %collective-permute-start = (bf16[512,768]{1,0:T(8,128)(2,1)S(1)}, bf16[512,768]{1,0:T(8,128)(2,1)S(1)}, u32[]{:S(2)}, u32[]{:S(2)}) collective-permute-start(bf16[512,768]{1,0:T(8,128)(2,1)S(1)} %copy-done.1), channel_id=1, source_target_pairs={{1,2},{2,1},{5,6},{6,5},{9,10},{10,9},{13,14},{14,13},{17,18},{18,... | collective-permute-start | bytes 2359304 | tf_op jit(solution)/shard_map/ppermute | solution.py:1115
  160.4 21.5 %copy-start.9 = (f32[8,768]{1,0:T(8,128)S(1)}, f32[8,768]{1,0:T(8,128)}, u32[]{:S(2)}) copy-start(f32[8,768]{1,0:T(8,128)} %get-tuple-element.95) | copy-start | bytes 73732
  181.9 54.6 %copy-start.10 = (f32[1,3072]{1,0:T(1,128)S(1)}, f32[1,3072]{1,0:T(1,128)}, u32[]{:S(2)}) copy-start(f32[1,3072]{1,0:T(1,128)} %get-tuple-element.98) | copy-start | bytes 36868
  237.1 66.8 %copy-start.2 = (bf16[512,768]{1,0:T(8,128)(2,1)S(1)}, bf16[512,768]{1,0:T(8,128)(2,1)}, u32[]{:S(2)}) copy-start(bf16[512,768]{1,0:T(8,128)(2,1)} %get-tuple-element.72) | copy-start | bytes 2359300
  237.1 68.8 %copy-start = (f32[512,768]{1,0:T(8,128)S(1)}, f32[512,768]{1,0:T(8,128)}, u32[]{:S(2)}) copy-start(f32[512,768]{1,0:T(8,128)} %get-tuple-element.88) | copy-start | bytes 4718596
  302.3 9.5 %copy-start.6 = (f32[152,128]{1,0:T(8,128)S(1)}, f32[152,128]{1,0:T(8,128)}, u32[]{:S(2)}) copy-start(f32[152,128]{1,0:T(8,128)} %get-tuple-element.99) | copy-start | bytes 233476
  304.0 13.3 %collective-permute-start.1 = (bf16[512,768]{1,0:T(8,128)(2,1)S(1)}, bf16[512,768]{1,0:T(8,128)(2,1)S(1)}, u32[]{:S(2)}, u32[]{:S(2)}) collective-permute-start(bf16[512,768]{1,0:T(8,128)(2,1)S(1)} %copy-done.2), channel_id=1, source_target_pairs={{1,2},{2,1},{5,6},{6,5},{9,10},{10,9},{13,14},{14,13},{17,18},{18,... | collective-permute-start | bytes 2359304 | tf_op jit(solution)/shard_map/ppermute | solution.py:1115
  306.9 18.9 %collective-permute-start.2 = (bf16[512,768]{1,0:T(8,128)(2,1)}, bf16[512,768]{1,0:T(8,128)(2,1)}, u32[]{:S(2)}, u32[]{:S(2)}) collective-permute-start(bf16[512,768]{1,0:T(8,128)(2,1)} %convert_element_type.26), channel_id=1, source_target_pairs={{1,2},{2,1},{5,6},{6,5},{9,10},{10,9},{13,14},{14,13},{17,18},{18,... | collective-permute-start | bytes 2359304 | tf_op jit(solution)/shard_map/ppermute | solution.py:1163
  318.2 10.0 %copy-start.5 = (f32[4,48,384]{2,1,0:T(8,128)S(1)}, f32[4,48,384]{2,1,0:T(8,128)}, u32[]{:S(2)}) copy-start(f32[4,48,384]{2,1,0:T(8,128)} %get-tuple-element.135) | copy-start | bytes 884740
  318.2 10.7 %copy-start.7 = (f32[2,48,384]{2,1,0:T(8,128)S(1)}, f32[2,48,384]{2,1,0:T(8,128)}, u32[]{:S(2)}) copy-start(f32[2,48,384]{2,1,0:T(8,128)} %get-tuple-element.136) | copy-start | bytes 442372
  318.2 11.4 %copy-start.8 = (f32[1,48,384]{2,1,0:T(8,128)S(1)}, f32[1,48,384]{2,1,0:T(8,128)}, u32[]{:S(2)}) copy-start(f32[1,48,384]{2,1,0:T(8,128)} %get-tuple-element.102) | copy-start | bytes 221188
  318.2 12.0 %copy-start.4 = (f32[1,48,1536]{2,1,0:T(8,128)S(1)}, f32[1,48,1536]{2,1,0:T(8,128)}, u32[]{:S(2)}) copy-start(f32[1,48,1536]{2,1,0:T(8,128)} %get-tuple-element.103) | copy-start | bytes 884740
  318.2 12.7 %copy-start.3 = (f32[1,48,1536]{2,1,0:T(8,128)S(1)}, f32[1,48,1536]{2,1,0:T(8,128)}, u32[]{:S(2)}) copy-start(f32[1,48,1536]{2,1,0:T(8,128)} %get-tuple-element.104) | copy-start | bytes 884740

commit v2 on v1

--- a/solution.py
+++ b/solution.py
@@ -129,6 +129,31 @@
     return pltpu.make_async_remote_copy(
         src_ref=src, dst_ref=dst, send_sem=send, recv_sem=recv, device_id=peer, device_id_type=MESH
     )
+
+
+class Trade:
+    def __init__(self, place, own, got, sems):
+        self.moved = place.moved
+        self.kept = pltpu.make_async_copy(own, got, sems.at[2])
+        self.swap = remote(own, got, sems.at[0], sems.at[1], place.transposed())
+
+    def start(self):
+        @pl.when(self.moved)
+        def _():
+            self.swap.start()
+
+        @pl.when(jnp.logical_not(self.moved))
+        def _():
+            self.kept.start()
+
+    def finish(self):
+        @pl.when(self.moved)
+        def _():
+            self.swap.wait()
+
+        @pl.when(jnp.logical_not(self.moved))
+        def _():
+            self.kept.wait()
 
 
 class Gather:
@@ -306,13 +331,19 @@
         Gather(place, shards[i], fulls[i], send.at[i], recv.at[i], local.at[i], i < wholes)
         for i in range(count)
     ]
-    for mover in movers:
+    for mover in movers[:2]:
         mover.stage1()
-    for index, step in enumerate(wavefront(movers)):
-        if step.__func__ is not Gather.stage1:
-            step()
-        if index == count:
+    steps = [s for s in wavefront(movers) if s.__func__ is not Gather.stage1]
+    late = [s for s in steps if s.__func__ is Gather.settle]
+    landed = 0
+    for index, step in enumerate([s for s in steps if s not in late] + late):
+        step()
+        if index == 1:
             tokens.forward()
+        if step.__func__ in (Gather.stage2, Gather.settle):
+            landed += 1
+            if landed + 1 < count:
+                movers[landed + 1].stage1()
     tokens.finish()
     for share in shares:
         share.finish()
@@ -516,10 +547,10 @@
 
 
 def scatter_kernel(subs, early, count, *refs):
-    pieces, parts, small = refs[:early], refs[early : early + count], refs[early + count]
-    refs = refs[early + count + 1 :]
-    totals, small_total = refs[: early + count], refs[early + count]
-    refs = refs[early + count + 1 :]
+    pieces, parts, (small, input_grad, input_low) = refs[:early], refs[early : early + count], refs[early + count :][:3]
+    refs = refs[early + count + 3 :]
+    totals, (small_total, result, traded, trade_sems) = refs[: early + count], refs[early + count :][:4]
+    refs = refs[early + count + 4 :]
     lasts, refs = refs[: 3 * (early + count)], refs[3 * (early + count) :]
     place = Place(subs)
     entry_barrier(place)
@@ -528,10 +559,12 @@
     ends = [Last(place, sources[i], totals[i], *lasts[3 * i : 3 * i + 3]) for i in range(early + count)]
     running, box, send, recv = refs[7 * count :]
     small_sum = Sum(place, small, running, box, send, recv)
+    trade = Trade(place, input_low, traded, trade_sems)
     for mover in movers:
         mover.stage1()
     for end in ends[:early]:
         end.start()
+    trade.start()
     extra = small_sum.stages()
     steps = []
     for time in range(count + 4):
@@ -551,16 +584,18 @@
     for mover in movers:
         mover.drain()
     small_total[...] = running[4]
-
-
-def scatter_gradients(subs, pieces, parts, small):
+    trade.finish()
+    result[...] = jnp.where(place.moved, traded[...].astype(F32), input_grad[...])
+
+
+def scatter_gradients(subs, pieces, parts, small, input_grad, input_low):
     early, count = len(pieces), len(parts)
     shaped = [as_shards(p) for p in parts]
     shapes = [(p.shape[0],) + p.shape[2:] for p in pieces]
     whole = [(p.shape[0], p.shape[4], p.shape[5] // 2) for p in shaped]
     outs = [jax.ShapeDtypeStruct(s, F32) for s in shapes + whole]
-    outs.append(jax.ShapeDtypeStruct(small.shape, F32))
-    scratch = []
+    outs += [jax.ShapeDtypeStruct(small.shape, F32), jax.ShapeDtypeStruct(input_grad.shape, F32)]
+    scratch = [pltpu.VMEM(input_low.shape, BF16), pltpu.SemaphoreType.DMA((3,))]
     for s in shapes + whole:
         scratch += last_scratch(s)
     for s in whole:
@@ -575,15 +610,15 @@
     results = pl.pallas_call(
         functools.partial(scatter_kernel, subs, early, count),
         out_shape=outs,
-        in_specs=[local] * early + [pl.BlockSpec(memory_space=pl.ANY)] * count + [local],
-        out_specs=[local] * (early + count + 1),
+        in_specs=[local] * early + [pl.BlockSpec(memory_space=pl.ANY)] * count + [local] * 3,
+        out_specs=[local] * (early + count + 2),
         scratch_shapes=scratch,
         compiler_params=pltpu.CompilerParams(
             collective_id=1, has_side_effects=True, vmem_limit_bytes=VMEM_LIMIT
         ),
         name="scatter_gradients",
-    )(*pieces, *shaped, small)
-    return results[:-1], results[-1]
+    )(*pieces, *shaped, small, input_grad, input_low)
+    return results[:-2], results[-2], results[-1]
 
 
 def head_lanes(half):
@@ -730,7 +765,7 @@
 
 def backward_kernel(
     subs, both, facts, probs, word, entity, keys, values, ctx, dctx, wq, wkv, d_one, down_part, up_part,
-    q_part, kv_part, input_grad, q_bias, v_bias, down_piece, up_piece,
+    q_part, kv_part, input_grad, q_bias, v_bias, down_piece, up_piece, input_low,
     column, turned_rows, pair_grad, pair_got, pair_send, pair_recv, *scratch,
 ):
     place = Place(subs)
@@ -842,6 +877,7 @@
             mover.drain()
         down_piece[...] = movers[0].mine[3]
         up_piece[...] = movers[1].mine[3]
+        input_low[...] = input_grad[...].astype(BF16)
 
 
 def attention_backward(subs, both, facts, probs, word, entity, keys, values, ctx, dctx, wq, wkv, d_one, down_part, up_part):
@@ -869,6 +905,7 @@
             jax.ShapeDtypeStruct((8, width), F32),
             piece,
             piece,
+            jax.ShapeDtypeStruct((rows, width), BF16),
         ],
         in_specs=[
             whole(both),
@@ -894,6 +931,7 @@
             behind(8),
             local,
             local,
+            local,
         ],
         scratch_shapes=[
             pltpu.VMEM((length, facts.shape[1]), jnp.int32),
@@ -914,13 +952,16 @@
 
 def ffn_forward_kernel(
     subs, both, ctx, w_out, up, down, unit_bias, out_bias, gain, shift, valid, grad_out,
-    active, slope, hidden_low, normal_one, inverse_one, output, d_two, sums, hidden, total,
+    active, slope, hidden_low, normal_one, inverse_one, output, d_two, sums, hidden, total, traded, sems,
 ):
     step = pl.program_id(0)
     place = Place(subs)
+    trade = Trade(place, grad_out, traded, sems)
 
     @pl.when(step == 0)
     def _():
+        entry_barrier(place)
+        trade.start()
         attn = dot_nt(ctx[...].T, w_out[...]) + out_bias[0:1].astype(F32)
         resid = both[place.c].astype(F32) + attn
         normal, inverse = normalize(resid)
@@ -948,7 +989,8 @@
         normal, inverse = normalize(resid)
         output[...] = (normal * gain[1:2].astype(F32) + shift[1:2].astype(F32)).astype(BF16)
         seen = valid[...]
-        grad = grad_out[...].astype(F32)
+        trade.finish()
+        grad = traded[...].astype(F32)
         back = norm_backward(grad, normal, inverse, gain[1:2].astype(F32))
         d_two[...] = back
         sums[2:3] = column_sum(seen * ffn * ffn)
@@ -979,7 +1021,8 @@
             jax.ShapeDtypeStruct((8, width), F32),
         ],
         in_specs=[whole(both), whole(ctx), whole(w_out), wide(width), wide(width), wide(1)]
-        + [whole(a) for a in (out_bias, gain, shift, valid, grad_out)],
+        + [whole(a) for a in (out_bias, gain, shift, valid)]
+        + [pl.BlockSpec(memory_space=pltpu.VMEM)],
         out_specs=[
             wide(rows),
             wide(rows),
@@ -990,8 +1033,15 @@
             fixed(rows, width),
             fixed(8, width),
         ],
-        scratch_shapes=[pltpu.VMEM((rows, width), F32), pltpu.VMEM((rows, width), F32)],
-        compiler_params=pltpu.CompilerParams(vmem_limit_bytes=VMEM_LIMIT),
+        scratch_shapes=[
+            pltpu.VMEM((rows, width), F32),
+            pltpu.VMEM((rows, width), F32),
+            pltpu.VMEM((rows, width), BF16),
+            pltpu.SemaphoreType.DMA((3,)),
+        ],
+        compiler_params=pltpu.CompilerParams(
+            collective_id=4, has_side_effects=True, vmem_limit_bytes=VMEM_LIMIT
+        ),
         cost_estimate=pl.CostEstimate(
             flops=2 * rows * width * (width + 2 * units),
             bytes_accessed=2 * width * (width + 2 * units) + 4 * rows * units,
@@ -1002,13 +1052,17 @@
 
 
 def ffn_backward_kernel(
-    d_two, hidden_low, active, slope, up, down, ctx, w_out, gain, normal_one, inverse_one,
-    up_part, down_part, bias_part, d_one, d_ctx, out_part, sums, d_low, d_turned, hidden_turned, total,
+    subs, result, d_two, hidden_low, active, slope, up, down, ctx, w_out, gain, normal_one, inverse_one,
+    up_part, down_part, bias_part, d_one, d_ctx, out_part, sums, output, d_low, d_turned, hidden_turned, total, sems,
 ):
     step = pl.program_id(0)
+    place = Place(subs)
+    trade = Trade(place, result, output, sems)
 
     @pl.when(step == 0)
     def _():
+        entry_barrier(place)
+        trade.start()
         low = d_two[...].astype(BF16)
         d_low[...] = low
         d_turned[...] = low.T
@@ -1034,16 +1088,17 @@
         sums[0:1] = column_sum(grad * normal)
         sums[1:2] = column_sum(grad)
         sums[2:3] = column_sum(low.astype(F32))
-
-
-def ffn_backward(d_two, hidden_low, active, slope, up, down, ctx, w_out, gain, normal_one, inverse_one):
+        trade.finish()
+
+
+def ffn_backward(subs, result, d_two, hidden_low, active, slope, up, down, ctx, w_out, gain, normal_one, inverse_one):
     rows, width = d_two.shape
     units = up.shape[1]
     whole = lambda a: pl.BlockSpec(a.shape, lambda i: (0,) * a.ndim, pipeline_mode=pl.Buffered(1))
     fixed = lambda r, w: pl.BlockSpec((r, w), lambda i: (0, 0), pipeline_mode=pl.Buffered(1))
     wide = lambda r: pl.BlockSpec((r, BLOCK), lambda i: (0, i))
     return pl.pallas_call(
-        ffn_backward_kernel,
+        functools.partial(ffn_backward_kernel, subs),
         grid=(units // BLOCK,),
         out_shape=[
             jax.ShapeDtypeStruct((width, units), BF16),
@@ -1053,8 +1108,9 @@
             jax.ShapeDtypeStruct((width, rows), BF16),
             jax.ShapeDtypeStruct((width, width), BF16),
             jax.ShapeDtypeStruct((8, width), F32),
-        ],
-        in_specs=[whole(d_two), whole(hidden_low), wide(rows), wide(rows), wide(width), wide(width)]
+            jax.ShapeDtypeStruct((rows, width), BF16),
+        ],
+        in_specs=[pl.BlockSpec(memory_space=pltpu.VMEM), whole(d_two), whole(hidden_low), wide(rows), wide(rows), wide(width), wide(width)]
         + [whole(a) for a in (ctx, w_out, gain, normal_one, inverse_one)],
         out_specs=[
             wide(width),
@@ -1064,21 +1120,25 @@
             fixed(width, rows),
             fixed(width, width),
             fixed(8, width),
+            pl.BlockSpec(memory_space=pl.ANY),
         ],
         scratch_shapes=[
             pltpu.VMEM((rows, width), BF16),
             pltpu.VMEM((width, rows), BF16),
             pltpu.VMEM((width, rows), BF16),
             pltpu.VMEM((rows, width), F32),
-        ],
-        compiler_params=pltpu.CompilerParams(vmem_limit_bytes=VMEM_LIMIT),
+            pltpu.SemaphoreType.DMA((3,)),
+        ],
+        compiler_params=pltpu.CompilerParams(
+            collective_id=5, has_side_effects=True, vmem_limit_bytes=VMEM_LIMIT
+        ),
         cost_estimate=pl.CostEstimate(
             flops=4 * rows * width * (width + 2 * units),
             bytes_accessed=2 * width * (3 * width + 4 * units) + 4 * rows * units,
             transcendentals=0,
         ),
         name="ffn_backward",
-    )(d_two, hidden_low, active, slope, up, down, ctx, w_out, gain, normal_one, inverse_one)
+    )(result, d_two, hidden_low, active, slope, up, down, ctx, w_out, gain, normal_one, inverse_one)
 
 
 def body(
@@ -1103,18 +1163,8 @@
     rank = lax.axis_index("tensor")
     subs = lax.axis_size("dp") // GRID
     core = (lax.axis_index("dp") // subs) % 2
-    moved = rank != core
     start = core * rows
     pairs = lax.axis_size("tensor")
-    trades = []
-    for d in range(lax.axis_size("dp")):
-        other = d + subs if (d // subs) % 2 == 0 else d - subs
-        y = 1 - (d // subs) % 2
-        trades.append((d * pairs + y, other * pairs + 1 - y))
-    def trade(own):
-        got = lax.ppermute(own, ("dp", "tensor"), trades)
-        return jnp.where(moved, got, own)
-
     shards = [
         query_weight,
         key_value_weight,
@@ -1146,28 +1196,23 @@
     facts = lax.dynamic_index_in_dim(pair_facts, rank, 0, keepdims=False)
 
     valid_own = lax.dynamic_slice_in_dim(facts[2], start, rows).astype(F32)[:, None]
-    grad_out, context_t = lax.optimization_barrier((grad_out, context_t))
     active, slope, hidden_low, normal_one, inverse_one, result, d_two, sums_two = ffn_forward(
         subs, both, context_t, w_out_t, w_up, w_down_t, ffn_bias_full[None], out_bias, ln_gain, ln_bias, valid_own,
-        trade(grad_out),
+        grad_out,
     )
-    output = trade(result)
-    up_part, down_part, ffn_bias_part, d_one, d_context_t, out_part, sums_one = ffn_backward(
-        d_two, hidden_low, active, slope, w_up, w_down_t, context_t, w_out_t, ln_gain, normal_one, inverse_one
+    up_part, down_part, ffn_bias_part, d_one, d_context_t, out_part, sums_one, output = ffn_backward(
+        subs, result, d_two, hidden_low, active, slope, w_up, w_down_t, context_t, w_out_t, ln_gain, normal_one, inverse_one
     )
 
-    query_part, kv_part, input_grad, q_bias, v_bias, down_piece, up_piece = attention_backward(
+    query_part, kv_part, input_grad, q_bias, v_bias, down_piece, up_piece, input_low = attention_backward(
         subs, both, pair_facts, probs, query_word, query_ent, keys, values, context_t, d_context_t, w_q, w_kv, d_one,
         down_part[None], up_part[None],
     )
-    returned = lax.ppermute(input_grad.astype(BF16), ("dp", "tensor"), trades)
-    input_grad = jnp.where(moved, returned.astype(F32), input_grad)
-
     small = jnp.concatenate([sums_one.reshape(-1), sums_two.reshape(-1), q_bias[:4].reshape(-1), v_bias[0], ffn_bias_part[0]])
     padded = -(-small.shape[0] // (8 * LANES)) * 8 * LANES
     small = jnp.pad(small, (0, padded - small.shape[0])).reshape(-1, LANES)
-    sums, small_sum = scatter_gradients(
-        subs, [down_piece, up_piece], [out_part[None], query_part, kv_part], small
+    sums, small_sum, input_grad = scatter_gradients(
+        subs, [down_piece, up_piece], [out_part[None], query_part, kv_part], small, input_grad, input_low
     )
     if subs > 1:
         sums = [

time: 333 us -> 313 us (0.940)
  the two profiles are of different devices: /device:TPU:1 before, /device:TPU:0 now
where the time goes in v2:
time: 313 us; the launch traced here: 310 us
  Pallas kernels  286 us (91%)
  local copies, waits for them, and re-layouts  16.3 us (5%)
  other arithmetic  6.15 us (2%)
    pallas_call x1, Pallas kernels, scatter_gradients(): pl.pallas_call(functools.partial(scatter_kernel, subs, early, count), out...  71.1 us
    pallas_call x1, Pallas kernels, attention_forward(): pl.pallas_call(functools.partial(forward_kernel, subs), grid=(pairs,), ou...  57.8 us
    pallas_call x1, Pallas kernels, gather_weights(): pl.pallas_call(functools.partial(gather_kernel, subs, count, wholes), out...  56.7 us
    pallas_call x1, Pallas kernels, attention_backward(): pl.pallas_call(functools.partial(backward_kernel, subs), grid=(pairs + 1,...  52.9 us
    pallas_call x1, Pallas kernels, ffn_forward(): pl.pallas_call(functools.partial(ffn_forward_kernel, subs), grid=(units /...  24.6 us
    pallas_call x1, Pallas kernels, ffn_backward(): pl.pallas_call(functools.partial(ffn_backward_kernel, subs), grid=(units...  22.6 us
    unnamed x30, local copies, waits for them, and re-layouts  6.4 us

profile of v2, /device:TPU:0, one launch (start us, length us, event | category | flops | bytes accessed | tf_op | source)
XLA Modules:
  0.0 309.6 jit_solution(15287603435204439613)
XLA Ops:
  0.7 0.7 pad_add_fusion
  1.4 0.6 pad.16.refs_7_
  2.0 0.7 reshape.89
  2.7 1.3 fusion.3.refs_6_
  4.0 56.7 %gather_weights.1 = (bf16[2,4,2,2,48,768]{5,4,3,2,1,0:T(8,128)(2,1)}, bf16[4,4,2,2,48,768]{5,4,3,2,1,0:T(8,128)(2,1)}, bf16[1,4,2,2,48,768]{5,4,3,2,1,0:T(8,128)...) custom-call(bf16[2,48,384]{2,1,0:T(8,128)(2,1)} %refs_0_.1, ...), custom_call_target="tpu_custom_call" | custom-call | tf_op jit(solution)/shard_map/gather_weights/pallas_call | solution.py:358
  60.8 0.8 fusion.4
  61.6 0.9 copy.30.valid
  62.5 57.8 %attention_forward.1 = (bf16[768,512]{1,0:T(8,128)(2,1)}, bf16[12,1024,512]{2,1,0:T(8,128)(2,1)}, bf16[512,768]{1,0:T(8,128)(2,1)}, bf16[512,768]{1,0:T(8,128)(2...) custom-call(bf16[2,512,768]{2,1,0:T(8,128)(2,1)} %get-tuple-element., ...), custom_call_target="tpu_custom_call", output_to_operand_aliasing={{6}: (5, {}), {7}: (6, {})} | custom-call | tf_op jit(solution)/shard_map/attention_forward/pallas_call | solution.py:720
  120.3 0.8 slice.77
  121.1 0.6 broadcast_in_dim_reshape.3.unit_bias
  121.7 24.6 %ffn_forward.1 = (bf16[512,3072]{1,0:T(8,128)(2,1)}, bf16[512,3072]{1,0:T(8,128)(2,1)}, bf16[512,768]{1,0:T(8,128)(2,1)}, f32[512,768]{1,0:T(8,128)}, f32[512,1]...) custom-call(bf16[2,512,768]{2,1,0:T(8,128)(2,1)} %get-tuple-element.60.both, ...), custom_call_target="tpu_custom_call" | custom-call | flops 5435817984 | bytes 16908288 | tf_op jit(solution)/shard_map/ffn_forward/pallas_call | solution.py:1010
  146.2 0.0 copy-start.7
  146.3 22.6 %ffn_backward.1 = (bf16[768,3072]{1,0:T(8,128)(2,1)}, bf16[768,3072]{1,0:T(8,128)(2,1)}, f32[1,3072]{1,0:T(1,128)}, f32[512,768]{1,0:T(8,128)}, bf16[768,512]{1,...) custom-call(bf16[512,768]{1,0:T(8,128)(2,1)} %get-tuple-element.71.result, ...), custom_call_target="tpu_custom_call" | custom-call | flops 10871635968 | bytes 28704768 | tf_op jit(solution)/shard_map/ffn_backward/pallas_call | solution.py:1100
  168.8 0.7 reshape.94
  169.6 0.0 copy-done.7
  169.6 0.0 copy-start.8
  169.6 52.9 %attention_backward.1 = (bf16[4,768,768]{2,1,0:T(8,128)(2,1)}, bf16[2,768,768]{2,1,0:T(8,128)(2,1)}, f32[512,768]{1,0:T(8,128)}, f32[8,768]{1,0:T(8,128)}, f32[8...) custom-call(bf16[2,512,768]{2,1,0:T(8,128)(2,1)} %get-tuple-element., ...), custom_call_target="tpu_custom_call" | custom-call | tf_op jit(solution)/shard_map/attention_backward/pallas_call | solution.py:897
  222.5 0.7 slice.79
  223.3 0.8 slice_reduce_fusion.1
  224.0 0.0 copy-done.8
  224.1 0.6 pad_bitcast_fusion.refs_5_
  224.7 71.1 %scatter_gradients.1 = (f32[1,48,1536]{2,1,0:T(8,128)}, f32[1,48,1536]{2,1,0:T(8,128)}, f32[1,48,384]{2,1,0:T(8,128)}, f32[4,48,384]{2,1,0:T(8,128)}, f32[2,48,3...) custom-call(bf16[1,4,48,1536]{3,2,1,0:T(8,128)(2,1)} %get-tuple-element.88.refs_0_, ...), custom_call_target="tpu_custom_call" | custom-call | tf_op jit(solution)/shard_map/scatter_gradients/pallas_call | solution.py:610
  295.8 0.0 copy-start
  295.8 0.9 slice_bitcast_fusion.2
  296.7 0.6 pad_maximum_fusion.2
  297.3 0.6 pad_maximum_fusion.1
  297.9 0.6 pad_maximum_fusion
  298.5 0.8 slice.82
  299.4 0.5 slice.99
  300.5 0.8 slice_bitcast_fusion
  301.4 0.1 reduce_sum.14
  301.4 0.1 reduce_sum.18
  301.6 0.5 divide_sqrt_fusion
  302.1 0.7 slice.84
  302.8 0.6 constant_dynamic-slice_fusion
  303.4 0.7 dynamic_slice.16
  304.1 0.0 copy-done.1
  304.1 0.9 copy.56
  305.0 0.0 copy-done
  305.0 1.1 copy.57
  306.2 0.7 copy.58
  306.9 0.0 copy-done.5
  306.9 0.7 copy.59
  307.5 0.6 copy.60
  308.2 0.0 copy-done.3
  308.2 0.7 copy.61
  308.9 0.0 copy-done.2
  308.9 0.7 copy.62
  (20 shorter events, 0.1 us)
Async XLA Ops:
  146.2 23.3 %copy-start.7 = (f32[8,768]{1,0:T(8,128)S(1)}, f32[8,768]{1,0:T(8,128)}, u32[]{:S(2)}) copy-start(f32[8,768]{1,0:T(8,128)} %get-tuple-element.94) | copy-start | bytes 73732
  169.6 54.5 %copy-start.8 = (f32[1,3072]{1,0:T(1,128)S(1)}, f32[1,3072]{1,0:T(1,128)}, u32[]{:S(2)}) copy-start(f32[1,3072]{1,0:T(1,128)} %get-tuple-element.97) | copy-start | bytes 36868
  224.7 79.4 %copy-start.1 = (bf16[512,768]{1,0:T(8,128)(2,1)S(1)}, bf16[512,768]{1,0:T(8,128)(2,1)}, u32[]{:S(2)}) copy-start(bf16[512,768]{1,0:T(8,128)(2,1)} %get-tuple-element.134) | copy-start | bytes 2359300
  295.8 9.2 %copy-start = (f32[512,768]{1,0:T(8,128)S(1)}, f32[512,768]{1,0:T(8,128)}, u32[]{:S(2)}) copy-start(f32[512,768]{1,0:T(8,128)} %get-tuple-element.135) | copy-start | bytes 4718596
  304.1 2.0 copy-start.4
  304.1 2.8 copy-start.5
  305.0 2.5 copy-start.6
  305.0 3.2 %copy-start.3 = (f32[1,48,1536]{2,1,0:T(8,128)S(1)}, f32[1,48,1536]{2,1,0:T(8,128)}, u32[]{:S(2)}) copy-start(f32[1,48,1536]{2,1,0:T(8,128)} %get-tuple-element.105) | copy-start | bytes 884740
  305.0 3.9 %copy-start.2 = (f32[1,48,1536]{2,1,0:T(8,128)S(1)}, f32[1,48,1536]{2,1,0:T(8,128)}, u32[]{:S(2)}) copy-start(f32[1,48,1536]{2,1,0:T(8,128)} %get-tuple-element.106) | copy-start | bytes 884740

commit v3 on v2

--- a/solution.py
+++ b/solution.py
@@ -18,7 +18,7 @@
 VMEM_LIMIT = 60 * 1024 * 1024
 
 
-BLOCK = 512
+BLOCK = 768
 TAIL = 0.34
 TAIL_Q = (
     0.1918165616711201,
@@ -101,6 +101,10 @@
     def sibling(self):
         return self.device(c=1 - self.c)
 
+    def plane(self):
+        x, y, c = (self.x, 1 - self.x), (self.y, 1 - self.y), (self.c, 1 - self.c)
+        return [self.device(x=x[k // 4], y=y[k // 2 % 2], c=c[k % 2]) for k in range(1, 8)]
+
     def across(self):
         return self.device(y=1 - self.y)
 
@@ -119,7 +123,7 @@
 def entry_barrier(place):
     barrier = pltpu.get_barrier_semaphore()
     peers = [place.z_peer(step) for step in (1, 2, 3)]
-    peers += [place.device(x=1 - place.x), place.across(), place.sibling(), place.transposed()]
+    peers += place.plane()
     for peer in peers:
         pl.semaphore_signal(barrier, inc=1, device_id=peer, device_id_type=MESH)
     pl.semaphore_wait(barrier, len(peers))
@@ -492,32 +496,63 @@
     def __init__(self, place, source, total, box, send, recv):
         self.place, self.source, self.total = place, source, total
         self.box, self.send, self.recv = box, send, recv
+        p = place
+        flip = p.z + 1 - 2 * (p.z % 2)
+        self.peers = (p.device(x=1 - p.x), p.across(), p.device(z=flip), p.device(z=p.turns[2]), p.sibling())
+
+    def term(self, index):
+        return self.source if index == 0 else self.total.at[index - 1]
+
+    def exchange(self, index):
+        return remote(
+            self.term(index), self.box.at[index], self.send.at[index], self.recv.at[index], self.peers[index]
+        )
 
     def hop(self, index):
-        p = self.place
-        flip = p.z + 1 - 2 * (p.z % 2)
-        far = (p.z + 2) % 4
-        peers = (p.sibling(), p.device(x=1 - p.x), p.device(y=1 - p.y), p.device(z=flip), p.device(z=far))
-        if index < 5:
-            src = self.source if index == 0 else self.total.at[index - 1]
-            step = remote(src, self.box.at[index], self.send.at[index], self.recv.at[index], peers[index])
+        self.exchange(index).start()
+
+    def land(self, index):
+        self.exchange(index).wait()
+        self.total[index] = self.term(index)[...] + self.box[index]
+
+
+class PlaneSum:
+    def __init__(self, place, source, middle, plane, line, send, recv):
+        self.place, self.source, self.middle = place, source, middle
+        self.plane, self.line, self.send, self.recv = plane, line, send, recv
+        p = place
+        spot = (p.x * 2 + p.y) * 2 + p.c
+        self.first = [
+            remote(source, plane.at[spot], send.at[k], recv.at[k], peer) for k, peer in enumerate(p.plane())
+        ]
+        self.second = [
+            remote(middle, line.at[p.z], send.at[6 + k], recv.at[6 + k], p.z_peer(k)) for k in (1, 2, 3)
+        ]
+        self.spot = spot
+
+    def start(self):
+        for step in self.first:
             step.start()
-            self.flying = step
-
-    def land(self, index):
-        self.flying.wait()
-        src = self.source if index == 0 else self.total.at[index - 1]
-        self.total[index] = src[...] + self.box[index]
-
-    def stages(self):
-        def first():
-            self.hop(0)
-
-        def later(index):
-            self.land(index)
-            self.hop(index + 1)
-
-        return [first] + [functools.partial(later, i) for i in range(5)]
+        self.plane[self.spot] = self.source[...]
+
+    def turn(self):
+        for step in self.first:
+            step.wait()
+        total = self.plane[0]
+        for k in range(1, 8):
+            total = total + self.plane[k]
+        self.middle[...] = total
+        for step in self.second:
+            step.start()
+        self.line[self.place.z] = total
+
+    def finish(self):
+        for step in self.second:
+            step.wait()
+        total = self.line[0]
+        for k in range(1, 4):
+            total = total + self.line[k]
+        return total
 
 
 def scatter_scratch(shape):
@@ -547,8 +582,9 @@
 
 
 def scatter_kernel(subs, early, count, *refs):
-    pieces, parts, (small, input_grad, input_low) = refs[:early], refs[early : early + count], refs[early + count :][:3]
-    refs = refs[early + count + 3 :]
+    pieces, parts, smalls = refs[:early], refs[early : early + count], refs[early + count :][:2]
+    input_grad, input_low = refs[early + count + 2 :][:2]
+    refs = refs[early + count + 4 :]
     totals, (small_total, result, traded, trade_sems) = refs[: early + count], refs[early + count :][:4]
     refs = refs[early + count + 4 :]
     lasts, refs = refs[: 3 * (early + count)], refs[3 * (early + count) :]
@@ -557,68 +593,96 @@
     movers = [Scatter(place, parts[i], *refs[7 * i : 7 * i + 7]) for i in range(count)]
     sources = list(pieces) + [mover.mine.at[3] for mover in movers]
     ends = [Last(place, sources[i], totals[i], *lasts[3 * i : 3 * i + 3]) for i in range(early + count)]
-    running, box, send, recv = refs[7 * count :]
-    small_sum = Sum(place, small, running, box, send, recv)
+    small, *boxes = refs[7 * count :]
+    small[...] = smalls[0][...]
+    small[4:5] = smalls[1][0:1]
+    small_sum = PlaneSum(place, small, *boxes)
     trade = Trade(place, input_low, traded, trade_sems)
+    small_sum.start()
     for mover in movers:
         mover.stage1()
+    small_sum.turn()
     for end in ends[:early]:
         end.start()
-    trade.start()
-    extra = small_sum.stages()
-    steps = []
-    for time in range(count + 4):
+    for time in range(count + 2):
         for index in range(count):
             stage = time - index
-            if 0 <= stage < 5:
-                mover, end = movers[index], ends[early + index]
-                steps.append((mover.stage2, mover.stage3, mover.stage4, end.start, end.finish)[stage])
-    for index, step in enumerate(steps):
-        if index < len(extra):
-            extra[index]()
-        step()
-    for step in extra[len(steps) :]:
-        step()
+            if 0 <= stage < 3:
+                mover = movers[index]
+                (mover.stage2, mover.stage3, mover.stage4)[stage]()
+                if stage == 1 and index == count - 1:
+                    trade.start()
+                if stage == 2:
+                    ends[early + index].start()
+    small_total[...] = small_sum.finish()
+    for end in ends[early:]:
+        end.finish()
     for end in ends[:early]:
         end.finish()
     for mover in movers:
         mover.drain()
-    small_total[...] = running[4]
     trade.finish()
     result[...] = jnp.where(place.moved, traded[...].astype(F32), input_grad[...])
 
 
-def scatter_gradients(subs, pieces, parts, small, input_grad, input_low):
+def scatter_gradients(subs, pieces, parts, smalls, input_grad, input_low):
     early, count = len(pieces), len(parts)
     shaped = [as_shards(p) for p in parts]
     shapes = [(p.shape[0],) + p.shape[2:] for p in pieces]
     whole = [(p.shape[0], p.shape[4], p.shape[5] // 2) for p in shaped]
     outs = [jax.ShapeDtypeStruct(s, F32) for s in shapes + whole]
-    outs += [jax.ShapeDtypeStruct(small.shape, F32), jax.ShapeDtypeStruct(input_grad.shape, F32)]
+    stack = smalls[0].shape
+    outs += [jax.ShapeDtypeStruct(stack, F32), jax.ShapeDtypeStruct(input_grad.shape, F32)]
     scratch = [pltpu.VMEM(input_low.shape, BF16), pltpu.SemaphoreType.DMA((3,))]
     for s in shapes + whole:
         scratch += last_scratch(s)
     for s in whole:
         scratch += scatter_scratch(s)
     scratch += [
-        pltpu.VMEM((5,) + small.shape, F32),
-        pltpu.VMEM((5,) + small.shape, F32),
-        pltpu.SemaphoreType.DMA((5,)),
-        pltpu.SemaphoreType.DMA((5,)),
+        pltpu.VMEM(stack, F32),
+        pltpu.VMEM(stack, F32),
+        pltpu.VMEM((8,) + stack, F32),
+        pltpu.VMEM((4,) + stack, F32),
+        pltpu.SemaphoreType.DMA((10,)),
+        pltpu.SemaphoreType.DMA((10,)),
     ]
     local = pl.BlockSpec(memory_space=pltpu.VMEM)
     results = pl.pallas_call(
         functools.partial(scatter_kernel, subs, early, count),
         out_shape=outs,
-        in_specs=[local] * early + [pl.BlockSpec(memory_space=pl.ANY)] * count + [local] * 3,
+        in_specs=[local] * early + [pl.BlockSpec(memory_space=pl.ANY)] * count + [local] * 4,
         out_specs=[local] * (early + count + 2),
         scratch_shapes=scratch,
         compiler_params=pltpu.CompilerParams(
             collective_id=1, has_side_effects=True, vmem_limit_bytes=VMEM_LIMIT
         ),
         name="scatter_gradients",
-    )(*pieces, *shaped, small, input_grad, input_low)
+    )(*pieces, *shaped, *smalls, input_grad, input_low)
     return results[:-2], results[-2], results[-1]
+
+
+def finish_kernel(place_of, stack, biases, query, kv, up, grad, out, gains, shifts, out_bias, attn_bias, *results):
+    place = place_of()
+    for i, ref in enumerate((gains, shifts, out_bias)):
+        ref[0:1] = stack[i : i + 1]
+        ref[1:2] = stack[12 + i : 13 + i]
+    cols = attn_bias.shape[1]
+    mine = pl.ds(pl.multiple_of(place.y * cols, LANES), cols)
+    attn_bias[...] = biases[0:5, mine]
+    for source, target in zip((query, kv, up, grad, out), results):
+        target[...] = source[...]
+
+
+def finish(subs, stack, biases, cols, arrays):
+    width = stack.shape[1]
+    shapes = [(2, width)] * 3 + [(5, cols)]
+    outs = [jax.ShapeDtypeStruct(s, F32) for s in shapes] + [jax.ShapeDtypeStruct(a.shape, a.dtype) for a in arrays]
+    return pl.pallas_call(
+        functools.partial(finish_kernel, functools.partial(Place, subs)),
+        out_shape=outs,
+        compiler_params=pltpu.CompilerParams(vmem_limit_bytes=VMEM_LIMIT),
+        name="finish",
+    )(stack, biases, *arrays)
 
 
 def head_lanes(half):
@@ -764,21 +828,29 @@
 
 
 def backward_kernel(
-    subs, both, facts, probs, word, entity, keys, values, ctx, dctx, wq, wkv, d_one, down_part, up_part,
-    q_part, kv_part, input_grad, q_bias, v_bias, down_piece, up_piece, input_low,
-    column, turned_rows, pair_grad, pair_got, pair_send, pair_recv, *scratch,
+    subs, both, facts, probs, word, entity, keys, values, ctx, dctx, wq, wkv, d_one, sums_one, sums_two, unit_sums,
+    down_part, up_part, q_part, kv_part, input_grad, q_bias, v_bias, down_piece, up_piece, input_low, sums,
+    column, turned_rows, pair_grad, pair_got, pair_send, pair_recv, small, running, box, sum_send, sum_recv, *scratch,
 ):
     place = Place(subs)
     step = pl.program_id(0)
     pairs = pl.num_programs(0) - 1
     rows = word.shape[0]
     movers = [Scatter(place, down_part, *scratch[:7]), Scatter(place, up_part, *scratch[7:])]
+    small_sum = Sum(place, small, running, box, sum_send, sum_recv)
     own = pl.ds(pl.multiple_of(place.c * rows, LANES), rows)
     other = pl.ds(pl.multiple_of((1 - place.c) * rows, LANES), rows)
 
     @pl.when(step == 0)
     def _():
         entry_barrier(place)
+        wide = small.shape[1]
+        small[0:8] = sums_one[...]
+        small[8:16] = sums_two[...]
+        small[16:24] = jnp.zeros_like(small[16:24])
+        for i in range(unit_sums.shape[1] // wide):
+            small[16 + i : 17 + i] = unit_sums[:, i * wide : (i + 1) * wide]
+        small_sum.hop(0)
         for mover in movers:
             mover.stage1()
         column[...] = facts[place.y].T
@@ -787,14 +859,30 @@
 
     @pl.when(step == 1)
     def _():
+        small_sum.land(0)
+        small_sum.hop(1)
         movers[0].stage2()
 
     @pl.when(step == 2)
     def _():
+        small_sum.land(1)
+        small_sum.hop(2)
         movers[1].stage2()
 
+    @pl.when(step == 3)
+    def _():
+        small_sum.land(2)
+        small_sum.hop(3)
+
+    @pl.when(step == 4)
+    def _():
+        small_sum.land(3)
+        small_sum.hop(4)
+
     @pl.when(step == 5)
     def _():
+        small_sum.land(4)
+        sums[...] = running[4]
         movers[0].stage3()
 
     @pl.when(step < pairs)
@@ -850,6 +938,7 @@
         input_grad[...] += dot_nt(query_grad, weights)
         part = dot_nn(turned_rows[...], query_grad).astype(BF16)
         sums = column_sum(query_grad.astype(F32))
+        q_bias[...] = jnp.zeros_like(q_bias)
         for m in range(4):
             span = slice(m * LANES, (m + 1) * LANES)
             q_part[m] = part[:, span]
@@ -867,6 +956,7 @@
         part = dot_nn(turned_rows[...], grad).astype(BF16)
         kv_part[0] = part[:, :LANES]
         kv_part[1] = part[:, LANES:]
+        v_bias[...] = jnp.zeros_like(v_bias)
         v_bias[0:1] = column_sum(grad[:, LANES:].astype(F32))
 
     @pl.when(step == pairs)
@@ -880,7 +970,9 @@
         input_low[...] = input_grad[...].astype(BF16)
 
 
-def attention_backward(subs, both, facts, probs, word, entity, keys, values, ctx, dctx, wq, wkv, d_one, down_part, up_part):
+def attention_backward(
+    subs, both, facts, probs, word, entity, keys, values, ctx, dctx, wq, wkv, d_one, smalls, down_part, up_part
+):
     _, rows, width = both.shape
     length = 2 * rows
     pairs = width // LANES
@@ -906,6 +998,7 @@
             piece,
             piece,
             jax.ShapeDtypeStruct((rows, width), BF16),
+            jax.ShapeDtypeStruct((24, width), F32),
         ],
         in_specs=[
             whole(both),
@@ -920,15 +1013,16 @@
             q_cols,
             kv_cols,
             whole(d_one),
-            anywhere,
-            anywhere,
-        ],
+        ]
+        + [whole(a) for a in smalls]
+        + [anywhere, anywhere],
         out_specs=[
             q_cols,
             kv_cols,
             pl.BlockSpec((rows, width), lambda i: (0, 0), pipeline_mode=pl.Buffered(1)),
             block(8),
             behind(8),
+            local,
             local,
             local,
             local,
@@ -940,6 +1034,11 @@
             pltpu.VMEM((pairs, rows, 2 * LANES), BF16),
             pltpu.SemaphoreType.DMA((pairs,)),
             pltpu.SemaphoreType.DMA((pairs,)),
+            pltpu.VMEM((24, width), F32),
+            pltpu.VMEM((5, 24, width), F32),
+            pltpu.VMEM((5, 24, width), F32),
+            pltpu.SemaphoreType.DMA((5,)),
+            pltpu.SemaphoreType.DMA((5,)),
         ]
         + scatter_scratch(shape)
         + scatter_scratch(shape),
@@ -947,15 +1046,19 @@
             collective_id=3, has_side_effects=True, vmem_limit_bytes=VMEM_LIMIT
         ),
         name="attention_backward",
-    )(both, facts, probs, word, entity, keys, values, ctx, dctx, wq, wkv, d_one, as_shards(down_part), as_shards(up_part))
+    )(
+        both, facts, probs, word, entity, keys, values, ctx, dctx, wq, wkv, d_one, *smalls,
+        as_shards(down_part), as_shards(up_part),
+    )
 
 
 def ffn_forward_kernel(
-    subs, both, ctx, w_out, up, down, unit_bias, out_bias, gain, shift, valid, grad_out,
-    active, slope, hidden_low, normal_one, inverse_one, output, d_two, sums, hidden, total, traded, sems,
+    subs, both, facts, ctx, w_out, up, down, biases, out_bias, gain, shift, grad_out,
+    active, slope, hidden_low, normal_one, inverse_one, output, d_two, sums, hidden, total, traded, valid, sems,
 ):
     step = pl.program_id(0)
     place = Place(subs)
+    rows = both.shape[1]
     trade = Trade(place, grad_out, traded, sems)
 
     @pl.when(step == 0)
@@ -971,11 +1074,19 @@
         normal_one[...] = normal
         inverse_one[...] = inverse
         total[...] = jnp.zeros_like(total)
-        seen = valid[...]
+        own = pl.ds(pl.multiple_of(place.c * rows, LANES), rows)
+        seen = facts[place.y, :, own].T[:, 2:3].astype(F32)
+        valid[...] = seen
         sums[0:1] = column_sum(seen * resid * resid)
         sums[1:2] = column_sum(seen * attn * attn)
 
-    pre = dot_nn(hidden_low[...], up[...]) + unit_bias[...]
+    span = biases.shape[2]
+    across = pl.num_programs(0) // 2
+    lines = BLOCK // span
+    half = step // across
+    line = 5 + lines * (step % across)
+    bias = jnp.concatenate([biases[half, pl.ds(line + i, 1), :] for i in range(lines)], axis=1)
+    pre = dot_nn(hidden_low[...], up[...]) + bias
     act, rise = gelu_pair(pre)
     act = act.astype(BF16)
     active[...] = act
@@ -1001,7 +1112,7 @@
         sums[7:8] = jnp.zeros_like(sums[7:8]) + jnp.sum(seen) * (1.0 / seen.shape[0])
 
 
-def ffn_forward(subs, both, ctx, w_out, up, down, unit_bias, out_bias, gain, shift, valid, grad_out):
+def ffn_forward(subs, both, facts, ctx, w_out, up, down, biases, out_bias, gain, shift, grad_out):
     _, rows, width = both.shape
     units = up.shape[1]
     whole = lambda a: pl.BlockSpec(a.shape, lambda i: (0,) * a.ndim, pipeline_mode=pl.Buffered(1))
@@ -1020,8 +1131,8 @@
             jax.ShapeDtypeStruct((rows, width), F32),
             jax.ShapeDtypeStruct((8, width), F32),
         ],
-        in_specs=[whole(both), whole(ctx), whole(w_out), wide(width), wide(width), wide(1)]
-        + [whole(a) for a in (out_bias, gain, shift, valid)]
+        in_specs=[whole(both), whole(facts), whole(ctx), whole(w_out), wide(width), wide(width)]
+        + [whole(a) for a in (biases, out_bias, gain, shift)]
         + [pl.BlockSpec(memory_space=pltpu.VMEM)],
         out_specs=[
             wide(rows),
@@ -1037,6 +1148,7 @@
             pltpu.VMEM((rows, width), F32),
             pltpu.VMEM((rows, width), F32),
             pltpu.VMEM((rows, width), BF16),
+            pltpu.VMEM((rows, 1), F32),
             pltpu.SemaphoreType.DMA((3,)),
         ],
         compiler_params=pltpu.CompilerParams(
@@ -1048,7 +1160,7 @@
             transcendentals=rows * units,
         ),
         name="ffn_forward",
-    )(both, ctx, w_out, up, down, unit_bias, out_bias, gain, shift, valid, grad_out)
+    )(both, facts, ctx, w_out, up, down, biases, out_bias, gain, shift, grad_out)
 
 
 def ffn_backward_kernel(
@@ -1162,9 +1274,6 @@
     length = segment.shape[0]
     rank = lax.axis_index("tensor")
     subs = lax.axis_size("dp") // GRID
-    core = (lax.axis_index("dp") // subs) % 2
-    start = core * rows
-    pairs = lax.axis_size("tensor")
     shards = [
         query_weight,
         key_value_weight,
@@ -1178,7 +1287,6 @@
             lax.all_gather(s, "dp", axis=1, tiled=True, axis_index_groups=groups) for s in shards
         ]
     shards = [shards[1], shards[0]] + shards[2:]
-    units = pairs * ffn_bias.shape[0]
     cols = attn_bias.shape[1]
     bias_rows = jnp.concatenate([attn_bias, ffn_bias.reshape(-1, cols)]).astype(F32)
     used = bias_rows.shape[0]
@@ -1192,56 +1300,53 @@
         subs, both, w_q, w_kv, biases, pair_facts, w_up, w_down_t
     )
     w_up, w_down_t = as_matrix(w_up)[0], as_matrix(w_down_t)[0]
-    ffn_bias_full = biases[:, 5:used].reshape(units)
-    facts = lax.dynamic_index_in_dim(pair_facts, rank, 0, keepdims=False)
-
-    valid_own = lax.dynamic_slice_in_dim(facts[2], start, rows).astype(F32)[:, None]
     active, slope, hidden_low, normal_one, inverse_one, result, d_two, sums_two = ffn_forward(
-        subs, both, context_t, w_out_t, w_up, w_down_t, ffn_bias_full[None], out_bias, ln_gain, ln_bias, valid_own,
-        grad_out,
+        subs, both, pair_facts, context_t, w_out_t, w_up, w_down_t, biases, out_bias, ln_gain, ln_bias, grad_out,
     )
     up_part, down_part, ffn_bias_part, d_one, d_context_t, out_part, sums_one, output = ffn_backward(
         subs, result, d_two, hidden_low, active, slope, w_up, w_down_t, context_t, w_out_t, ln_gain, normal_one, inverse_one
     )
 
-    query_part, kv_part, input_grad, q_bias, v_bias, down_piece, up_piece, input_low = attention_backward(
+    query_part, kv_part, input_grad, q_bias, v_bias, down_piece, up_piece, input_low, stack = attention_backward(
         subs, both, pair_facts, probs, query_word, query_ent, keys, values, context_t, d_context_t, w_q, w_kv, d_one,
-        down_part[None], up_part[None],
+        [sums_one, sums_two, ffn_bias_part], down_part[None], up_part[None],
     )
-    small = jnp.concatenate([sums_one.reshape(-1), sums_two.reshape(-1), q_bias[:4].reshape(-1), v_bias[0], ffn_bias_part[0]])
-    padded = -(-small.shape[0] // (8 * LANES)) * 8 * LANES
-    small = jnp.pad(small, (0, padded - small.shape[0])).reshape(-1, LANES)
-    sums, small_sum, input_grad = scatter_gradients(
-        subs, [down_piece, up_piece], [out_part[None], query_part, kv_part], small, input_grad, input_low
+    sums, bias_sum, input_grad = scatter_gradients(
+        subs,
+        [down_piece, up_piece],
+        [query_part, kv_part, out_part[None]],
+        [q_bias, v_bias],
+        input_grad,
+        input_low,
     )
     if subs > 1:
         sums = [
             lax.psum_scatter(s, "dp", scatter_dimension=1, tiled=True, axis_index_groups=groups)
             for s in sums
         ]
-        small_sum = lax.psum(small_sum, "dp", axis_index_groups=groups)
-    down_sum, up_sum, out_sum, query_sum, kv_sum = sums
-    flat = small_sum.reshape(-1)
-    norms = flat[: 16 * width].reshape(16, width)
-    gains, shifts, out_biases = (jnp.stack([norms[i], norms[12 + i]]) for i in range(3))
-    attn_biases = flat[16 * width : 21 * width].reshape(5, width)
-    ffn_biases = flat[21 * width : 21 * width + units]
-    squares = jnp.sum(norms[8:12], 1)
-    real = norms[15, 0] * rows
+        stack = lax.psum(stack, "dp", axis_index_groups=groups)
+        bias_sum = lax.psum(bias_sum, "dp", axis_index_groups=groups)
+    down_sum, up_sum, query_sum, kv_sum, out_sum = sums
     half = ffn_bias.shape[0]
+    gains, shifts, out_biases, attn_biases, query_sum, kv_sum, up_sum, input_grad, output = finish(
+        subs, stack, bias_sum, cols, [query_sum, kv_sum, up_sum, input_grad, output]
+    )
+    squares = jnp.sum(stack[8:12], 1)
+    real = stack[15, 0] * rows
+    lines = half // width
     return (
         output,
         input_grad,
         jnp.sqrt(squares / (real * width)),
         query_sum,
         kv_sum,
-        lax.dynamic_slice_in_dim(attn_biases, rank * cols, cols, 1),
+        attn_biases,
         out_sum[0].T,
         out_biases,
         gains,
         shifts,
         up_sum[0],
-        lax.dynamic_slice_in_dim(ffn_biases, rank * half, half, 0),
+        lax.dynamic_slice_in_dim(stack, 16 + rank * lines, lines, 0).reshape(half),
         down_sum[0].T,
     )
 

time: 313 us -> 288 us (0.920)
  local copies, waits for them, and re-layouts: 16.3 us -> 5.23 us
  Pallas kernels: 286 us -> 277 us
    pallas_call x1, Pallas kernels: 71.1 us -> 63 us  [scatter_gradients(): pl.pallas_call(functools.partial(scatter_kernel, subs, early, count), out...]
    unnamed x30 -> x6, local copies, waits for them, and re-layouts: 6.4 us -> 1.35 us
    pallas_call x0 -> x1, Pallas kernels: none -> 3.66 us  [finish(): pl.pallas_call(functools.partial(finish_kernel, functools.partial(Place,...]
    pallas_call x1, Pallas kernels: 57.8 us -> 54.4 us  [attention_forward(): pl.pallas_call(functools.partial(forward_kernel, subs), grid=(pairs,), ou...]
    slice x9 -> x1, local copies, waits for them, and re-layouts: 4.36 us -> 1.2 us  [body(): real = stack[15, 0] * rows]
where the time goes in v3:
time: 288 us; the launch traced here: 287 us
  Pallas kernels  277 us (96%)
  local copies, waits for them, and re-layouts  5.23 us (2%)
  other arithmetic  3.42 us (1%)
    pallas_call x1, Pallas kernels, scatter_gradients(): pl.pallas_call(functools.partial(scatter_kernel, subs, early, count), out...  63 us
    pallas_call x1, Pallas kernels, gather_weights(): pl.pallas_call(functools.partial(gather_kernel, subs, count, wholes), out...  56.8 us
    pallas_call x1, Pallas kernels, attention_forward(): pl.pallas_call(functools.partial(forward_kernel, subs), grid=(pairs,), ou...  54.4 us
    pallas_call x1, Pallas kernels, attention_backward(): pl.pallas_call(functools.partial(backward_kernel, subs), grid=(pairs + 1,...  52.3 us
    pallas_call x1, Pallas kernels, ffn_backward(): pl.pallas_call(functools.partial(ffn_backward_kernel, subs), grid=(units...  23.7 us
    pallas_call x1, Pallas kernels, ffn_forward(): pl.pallas_call(functools.partial(ffn_forward_kernel, subs), grid=(units /...  22.8 us

profile of v3, /device:TPU:0, one launch (start us, length us, event | category | flops | bytes accessed | tf_op | source)
XLA Modules:
  0.0 286.7 jit_solution(324713702552658565)
XLA Ops:
  0.6 0.7 reshape.46
  1.3 1.3 fusion.3.refs_6_
  2.7 0.7 pad_add_fusion
  3.4 0.6 pad.12.refs_7_
  4.0 56.8 %gather_weights.1 = (bf16[2,4,2,2,48,768]{5,4,3,2,1,0:T(8,128)(2,1)}, bf16[4,4,2,2,48,768]{5,4,3,2,1,0:T(8,128)(2,1)}, bf16[1,4,2,2,48,768]{5,4,3,2,1,0:T(8,128)...) custom-call(bf16[2,48,384]{2,1,0:T(8,128)(2,1)} %refs_0_.1, ...), custom_call_target="tpu_custom_call" | custom-call | tf_op jit(solution)/shard_map/gather_weights/pallas_call | solution.py:362
  60.8 54.4 %attention_forward.1 = (bf16[768,512]{1,0:T(8,128)(2,1)}, bf16[12,1024,512]{2,1,0:T(8,128)(2,1)}, bf16[512,768]{1,0:T(8,128)(2,1)}, bf16[512,768]{1,0:T(8,128)(2...) custom-call(bf16[2,512,768]{2,1,0:T(8,128)(2,1)} %get-tuple-element., ...), custom_call_target="tpu_custom_call", output_to_operand_aliasing={{6}: (5, {}), {7}: (6, {})} | custom-call | tf_op jit(solution)/shard_map/attention_forward/pallas_call | solution.py:784
  115.2 22.8 %ffn_forward.1 = (bf16[512,3072]{1,0:T(8,128)(2,1)}, bf16[512,3072]{1,0:T(8,128)(2,1)}, bf16[512,768]{1,0:T(8,128)(2,1)}, f32[512,768]{1,0:T(8,128)}, f32[512,1]...) custom-call(bf16[2,512,768]{2,1,0:T(8,128)(2,1)} %get-tuple-element.70.both, ...), custom_call_target="tpu_custom_call" | custom-call | flops 5435817984 | bytes 16908288 | tf_op jit(solution)/shard_map/ffn_forward/pallas_call | solution.py:1121
  138.1 23.7 %ffn_backward.1 = (bf16[768,3072]{1,0:T(8,128)(2,1)}, bf16[768,3072]{1,0:T(8,128)(2,1)}, f32[1,3072]{1,0:T(1,128)}, f32[512,768]{1,0:T(8,128)}, bf16[768,512]{1,...) custom-call(bf16[512,768]{1,0:T(8,128)(2,1)} %get-tuple-element.86.result, ...), custom_call_target="tpu_custom_call" | custom-call | flops 10871635968 | bytes 28704768 | tf_op jit(solution)/shard_map/ffn_backward/pallas_call | solution.py:1212
  161.8 52.3 %attention_backward.1 = (bf16[4,768,768]{2,1,0:T(8,128)(2,1)}, bf16[2,768,768]{2,1,0:T(8,128)(2,1)}, f32[512,768]{1,0:T(8,128)}, f32[8,768]{1,0:T(8,128)}, f32[8...) custom-call(bf16[2,512,768]{2,1,0:T(8,128)(2,1)} %get-tuple-element., ...), custom_call_target="tpu_custom_call" | custom-call | tf_op jit(solution)/shard_map/attention_backward/pallas_call | solution.py:989
  214.1 63.0 %scatter_gradients.1 = (f32[1,48,1536]{2,1,0:T(8,128)}, f32[1,48,1536]{2,1,0:T(8,128)}, f32[4,48,384]{2,1,0:T(8,128)}, f32[2,48,384]{2,1,0:T(8,128)}, f32[1,48,3...) custom-call(bf16[1,4,48,1536]{3,2,1,0:T(8,128)(2,1)} %get-tuple-element.101.refs_0_, ...), custom_call_target="tpu_custom_call" | custom-call | tf_op jit(solution)/shard_map/scatter_gradients/pallas_call | solution.py:650
  277.1 0.0 copy-start.1
  277.1 0.0 copy-start
  277.1 3.7 %finish.1 = (f32[2,768]{1,0:T(2,128)}, f32[2,768]{1,0:T(2,128)}, f32[2,768]{1,0:T(2,128)}, f32[5,384]{1,0:T(8,128)}, f32[4,48,384]{2,1,0:T(8,128)}, /*index=5*/f...) custom-call(f32[24,768]{1,0:T(8,128)} %get-tuple-element.100.stack, ...), custom_call_target="tpu_custom_call" | custom-call | tf_op jit(solution)/shard_map/finish/pallas_call | solution.py:680
  280.7 0.9 slice_reduce_fusion
  281.6 1.2 slice.7
  283.4 0.5 divide_sqrt_fusion
  284.0 0.7 constant_dynamic-slice_fusion
  284.7 0.6 reshape.51
  285.3 0.0 copy-done.1
  285.3 0.6 copy.34
  286.0 0.0 copy-done
  286.0 0.7 copy.35
Async XLA Ops:
  277.1 8.3 %copy-start.1 = (f32[1,48,384]{2,1,0:T(8,128)S(1)}, f32[1,48,384]{2,1,0:T(8,128)}, u32[]{:S(2)}) copy-start(f32[1,48,384]{2,1,0:T(8,128)} %get-tuple-element.121) | copy-start | bytes 221188
  277.1 8.9 %copy-start = (f32[1,48,1536]{2,1,0:T(8,128)S(1)}, f32[1,48,1536]{2,1,0:T(8,128)}, u32[]{:S(2)}) copy-start(f32[1,48,1536]{2,1,0:T(8,128)} %get-tuple-element.126) | copy-start | bytes 884740

commit v4 on v3

--- a/solution.py
+++ b/solution.py
@@ -92,11 +92,11 @@
     def z_peer(self, step):
         return self.device(z=(self.z + step) % 4)
 
-    def first(self):
-        return self.device(x=self.x1, y=self.y1)
-
-    def second(self):
-        return self.device(x=self.x2, y=self.y2)
+    def first(self, flat=False):
+        return self.across() if flat else self.device(x=self.x1, y=self.y1)
+
+    def second(self, flat=False):
+        return self.device(x=1 - self.x) if flat else self.device(x=self.x2, y=self.y2)
 
     def sibling(self):
         return self.device(c=1 - self.c)
@@ -111,7 +111,9 @@
     def transposed(self):
         return self.device(c=1 - self.c, y=1 - self.y)
 
-    def pieces(self):
+    def pieces(self, flat=False):
+        if flat:
+            return ((self.x, self.y), (self.x, 1 - self.y), (1 - self.x, self.y), (1 - self.x, 1 - self.y))
         return (
             (self.x, self.y),
             (self.x1, self.y1),
@@ -161,7 +163,8 @@
 
 
 class Gather:
-    def __init__(self, place, shard, full, send, recv, local=None, whole=True):
+    def __init__(self, place, shard, full, send, recv, local=None, whole=True, flat=False):
+        self.flat = flat
         self.place, self.shard, self.full, self.whole = place, shard, full, whole
         self.send, self.recv, self.local = send, recv, local
         self.w = full.shape[-1] // 2
@@ -206,9 +209,9 @@
 
     def spread(self):
         p = self.place
-        mine = self.piece(p.pieces()[0], p.c)
-        self.copy(3, mine, mine, p.first())
-        self.copy(4, mine, mine, p.second())
+        mine = self.piece(p.pieces(self.flat)[0], p.c)
+        self.copy(3, mine, mine, p.first(self.flat))
+        self.copy(4, mine, mine, p.second(self.flat))
         self.copy(6, mine, mine, p.sibling())
 
     def stage2(self):
@@ -217,22 +220,22 @@
 
     def stage3(self):
         p = self.place
-        got = self.piece(p.pieces()[1], p.c)
+        got = self.piece(p.pieces(self.flat)[1], p.c)
         self.arrive(3, got)
-        self.copy(5, got, got, p.second())
+        self.copy(5, got, got, p.second(self.flat))
         self.copy(7, got, got, p.sibling())
 
     def stage4(self):
         p = self.place
         for index, spot in ((4, 2), (5, 3)):
-            got = self.piece(p.pieces()[spot], p.c)
+            got = self.piece(p.pieces(self.flat)[spot], p.c)
             self.arrive(index, got)
             self.copy(index + 4, got, got, p.sibling())
 
     def stage5(self):
         p = self.place
-        spots = p.pieces()
-        for index, spot in ((6, 0), (7, 2), (8, 1), (9, 3)):
+        spots = p.pieces(self.flat)
+        for index, spot in ((6, 0), (7, 1 if self.flat else 2), (8, 2 if self.flat else 1), (9, 3)):
             self.arrive(index, self.piece(spots[spot], 1 - p.c))
         for index in range(3, 10):
             self.gone(index, self.piece(spots[0], p.c))
@@ -318,12 +321,20 @@
 
 
 def gather_kernel(subs, count, wholes, *refs):
-    shards, (rows, bias, facts) = refs[:count], refs[count : count + 3]
-    fulls, (both, biases, pair_facts) = refs[count + 3 : 2 * count + 3], refs[2 * count + 3 : 2 * count + 6]
-    send, recv, local, row_sems, share_sems = refs[2 * count + 6 :]
+    shards, (rows, bias_rows, unit_bias), columns = refs[:count], refs[count : count + 3], refs[count + 3 : count + 6]
+    fulls, (both, biases, pair_facts) = refs[count + 6 : 2 * count + 6], refs[2 * count + 6 : 2 * count + 9]
+    send, recv, local, row_sems, share_sems, bias, facts = refs[2 * count + 9 :]
     place = Place(subs)
     entry_barrier(place)
     tokens = Rows(place, rows, both, row_sems)
+    bias[...] = jnp.zeros_like(bias)
+    many, span = bias_rows.shape
+    bias[0:many] = bias_rows[...].astype(F32)
+    for i in range(unit_bias.shape[1] // span):
+        bias[many + i : many + i + 1] = unit_bias[:, i * span : (i + 1) * span].astype(F32)
+    facts[...] = jnp.zeros_like(facts)
+    for i in range(3):
+        facts[i : i + 1] = columns[i][...]
     shares = [
         Share(facts, pair_facts, place.c, place.sibling(), share_sems.at[0]),
         Share(bias, biases, place.y, place.across(), share_sems.at[1]),
@@ -353,16 +364,21 @@
         share.finish()
 
 
-def gather_weights(subs, shards, wholes, rows, bias, facts):
+def gather_weights(subs, shards, wholes, rows, bias_rows, unit_bias, columns):
     count = len(shards)
     outs = [
         jax.ShapeDtypeStruct((s.shape[0], 4, 2, 2, s.shape[1], 2 * s.shape[2]), BF16) for s in shards
     ]
-    outs += [jax.ShapeDtypeStruct((2,) + a.shape, a.dtype) for a in (rows, bias, facts)]
+    bias, facts = (16, bias_rows.shape[1]), (8, columns[0].shape[1])
+    outs += [
+        jax.ShapeDtypeStruct((2,) + rows.shape, rows.dtype),
+        jax.ShapeDtypeStruct((2,) + bias, F32),
+        jax.ShapeDtypeStruct((2,) + facts, jnp.int32),
+    ]
     results = pl.pallas_call(
         functools.partial(gather_kernel, subs, count, wholes),
         out_shape=outs,
-        in_specs=[pl.BlockSpec(memory_space=pltpu.VMEM)] * (count + 3),
+        in_specs=[pl.BlockSpec(memory_space=pltpu.VMEM)] * (count + 6),
         out_specs=[pl.BlockSpec(memory_space=pl.ANY)] * (count + 3),
         scratch_shapes=[
             pltpu.SemaphoreType.DMA((count, 10)),
@@ -370,12 +386,14 @@
             pltpu.SemaphoreType.DMA((count,)),
             pltpu.SemaphoreType.DMA((5,)),
             pltpu.SemaphoreType.DMA((2, 3)),
+            pltpu.VMEM(bias, F32),
+            pltpu.VMEM(facts, jnp.int32),
         ],
         compiler_params=pltpu.CompilerParams(
             collective_id=0, has_side_effects=True, vmem_limit_bytes=VMEM_LIMIT
         ),
         name="gather_weights",
-    )(*shards, rows, bias, facts)
+    )(*shards, rows, bias_rows, unit_bias, *columns)
     return results[:count], results[count:]
 
 
@@ -661,8 +679,18 @@
     return results[:-2], results[-2], results[-1]
 
 
-def finish_kernel(place_of, stack, biases, query, kv, up, grad, out, gains, shifts, out_bias, attn_bias, *results):
+def finish_kernel(place_of, rows, stack, biases, query, kv, up, grad, out, gains, shifts, out_bias, attn_bias, unit_bias, rms, *results):
     place = place_of()
+    width = stack.shape[1]
+    lines = unit_bias.shape[1] // width
+    for i in range(lines):
+        unit_bias[:, i * width : (i + 1) * width] = stack[pl.ds(16 + place.y * lines + i, 1), :]
+    real = jnp.mean(stack[15:16], 1, keepdims=True) * (rows * width)
+    lane = lax.broadcasted_iota(jnp.int32, (1, 4), 1)
+    squares = jnp.zeros((1, 4), F32)
+    for i in range(4):
+        squares = jnp.where(lane == i, jnp.sum(stack[8 + i : 9 + i], 1, keepdims=True), squares)
+    rms[...] = jnp.sqrt(squares / real)
     for i, ref in enumerate((gains, shifts, out_bias)):
         ref[0:1] = stack[i : i + 1]
         ref[1:2] = stack[12 + i : 13 + i]
@@ -673,12 +701,12 @@
         target[...] = source[...]
 
 
-def finish(subs, stack, biases, cols, arrays):
+def finish(subs, rows, stack, biases, cols, units, arrays):
     width = stack.shape[1]
-    shapes = [(2, width)] * 3 + [(5, cols)]
+    shapes = [(2, width)] * 3 + [(5, cols), (1, units), (1, 4)]
     outs = [jax.ShapeDtypeStruct(s, F32) for s in shapes] + [jax.ShapeDtypeStruct(a.shape, a.dtype) for a in arrays]
     return pl.pallas_call(
-        functools.partial(finish_kernel, functools.partial(Place, subs)),
+        functools.partial(finish_kernel, functools.partial(Place, subs), rows),
         out_shape=outs,
         compiler_params=pltpu.CompilerParams(vmem_limit_bytes=VMEM_LIMIT),
         name="finish",
@@ -1086,8 +1114,7 @@
     half = step // across
     line = 5 + lines * (step % across)
     bias = jnp.concatenate([biases[half, pl.ds(line + i, 1), :] for i in range(lines)], axis=1)
-    pre = dot_nn(hidden_low[...], up[...]) + bias
-    act, rise = gelu_pair(pre)
+    act, rise = gelu_pair(dot_nn(hidden_low[...], up[...]) + bias)
     act = act.astype(BF16)
     active[...] = act
     slope[...] = rise.astype(BF16)
@@ -1288,12 +1315,8 @@
         ]
     shards = [shards[1], shards[0]] + shards[2:]
     cols = attn_bias.shape[1]
-    bias_rows = jnp.concatenate([attn_bias, ffn_bias.reshape(-1, cols)]).astype(F32)
-    used = bias_rows.shape[0]
-    bias_rows = jnp.pad(bias_rows, ((0, -used % 16), (0, 0)))
-    facts = jnp.pad(jnp.stack([segment, entity, valid_mask]), ((0, 5), (0, 0)))
     (w_kv, w_q, w_out_t, w_up, w_down_t), (both, biases, pair_facts) = gather_weights(
-        subs, shards, 3, layer_input, bias_rows, facts
+        subs, shards, 3, layer_input, attn_bias, ffn_bias[None], [segment[None], entity[None], valid_mask[None]]
     )
     w_kv, w_q, w_out_t = as_matrix(w_kv), as_matrix(w_q), as_matrix(w_out_t)[0]
     context_t, probs, query_word, query_ent, keys, values, w_up, w_down_t = attention_forward(
@@ -1328,16 +1351,13 @@
         bias_sum = lax.psum(bias_sum, "dp", axis_index_groups=groups)
     down_sum, up_sum, query_sum, kv_sum, out_sum = sums
     half = ffn_bias.shape[0]
-    gains, shifts, out_biases, attn_biases, query_sum, kv_sum, up_sum, input_grad, output = finish(
-        subs, stack, bias_sum, cols, [query_sum, kv_sum, up_sum, input_grad, output]
+    gains, shifts, out_biases, attn_biases, unit_biases, rms, query_sum, kv_sum, up_sum, input_grad, output = finish(
+        subs, rows, stack, bias_sum, cols, half, [query_sum, kv_sum, up_sum, input_grad, output]
     )
-    squares = jnp.sum(stack[8:12], 1)
-    real = stack[15, 0] * rows
-    lines = half // width
     return (
         output,
         input_grad,
-        jnp.sqrt(squares / (real * width)),
+        rms[0],
         query_sum,
         kv_sum,
         attn_biases,
@@ -1346,7 +1366,7 @@
         gains,
         shifts,
         up_sum[0],
-        lax.dynamic_slice_in_dim(stack, 16 + rank * lines, lines, 0).reshape(half),
+        unit_biases[0],
         down_sum[0].T,
     )
 

time: 288 us -> 283 us (0.983)
  no operation moved by 1% of the time
where the time goes in v4:
time: 283 us; the launch traced here: 281 us
  Pallas kernels  277 us (98%)
    pallas_call x1, Pallas kernels, scatter_gradients(): pl.pallas_call(functools.partial(scatter_kernel, subs, early, count), out...  62.9 us
    pallas_call x1, Pallas kernels, gather_weights(): pl.pallas_call(functools.partial(gather_kernel, subs, count, wholes), out...  56.8 us
    pallas_call x1, Pallas kernels, attention_forward(): pl.pallas_call(functools.partial(forward_kernel, subs), grid=(pairs,), ou...  54.5 us
    pallas_call x1, Pallas kernels, attention_backward(): pl.pallas_call(functools.partial(backward_kernel, subs), grid=(pairs + 1,...  52.3 us
    pallas_call x1, Pallas kernels, ffn_backward(): pl.pallas_call(functools.partial(ffn_backward_kernel, subs), grid=(units...  23.7 us
    pallas_call x1, Pallas kernels, ffn_forward(): pl.pallas_call(functools.partial(ffn_forward_kernel, subs), grid=(units /...  22.8 us

profile of v4, /device:TPU:0, one launch (start us, length us, event | category | flops | bytes accessed | tf_op | source)
XLA Modules:
  0.0 281.4 jit_solution(9866224036904399615)
XLA Ops:
  0.6 1.3 broadcast_in_dim.24.refs_7_
  1.9 56.8 %gather_weights.1 = (bf16[2,4,2,2,48,768]{5,4,3,2,1,0:T(8,128)(2,1)}, bf16[4,4,2,2,48,768]{5,4,3,2,1,0:T(8,128)(2,1)}, bf16[1,4,2,2,48,768]{5,4,3,2,1,0:T(8,128)...) custom-call(bf16[2,48,384]{2,1,0:T(8,128)(2,1)} %refs_0_.1, ...), custom_call_target="tpu_custom_call" | custom-call | tf_op jit(solution)/shard_map/gather_weights/pallas_call | solution.py:378
  58.8 54.5 %attention_forward.1 = (bf16[768,512]{1,0:T(8,128)(2,1)}, bf16[12,1024,512]{2,1,0:T(8,128)(2,1)}, bf16[512,768]{1,0:T(8,128)(2,1)}, bf16[512,768]{1,0:T(8,128)(2...) custom-call(bf16[2,512,768]{2,1,0:T(8,128)(2,1)} %get-tuple-element., ...), custom_call_target="tpu_custom_call", output_to_operand_aliasing={{6}: (5, {}), {7}: (6, {})} | custom-call | tf_op jit(solution)/shard_map/attention_forward/pallas_call | solution.py:812
  113.3 22.8 %ffn_forward.1 = (bf16[512,3072]{1,0:T(8,128)(2,1)}, bf16[512,3072]{1,0:T(8,128)(2,1)}, bf16[512,768]{1,0:T(8,128)(2,1)}, f32[512,768]{1,0:T(8,128)}, f32[512,1]...) custom-call(bf16[2,512,768]{2,1,0:T(8,128)(2,1)} %get-tuple-element.72.both, ...), custom_call_target="tpu_custom_call" | custom-call | flops 5435817984 | bytes 16908288 | tf_op jit(solution)/shard_map/ffn_forward/pallas_call | solution.py:1148
  136.1 23.7 %ffn_backward.1 = (bf16[768,3072]{1,0:T(8,128)(2,1)}, bf16[768,3072]{1,0:T(8,128)(2,1)}, f32[1,3072]{1,0:T(1,128)}, f32[512,768]{1,0:T(8,128)}, bf16[768,512]{1,...) custom-call(bf16[512,768]{1,0:T(8,128)(2,1)} %get-tuple-element.88.result, ...), custom_call_target="tpu_custom_call" | custom-call | flops 10871635968 | bytes 28704768 | tf_op jit(solution)/shard_map/ffn_backward/pallas_call | solution.py:1239
  159.8 52.3 %attention_backward.1 = (bf16[4,768,768]{2,1,0:T(8,128)(2,1)}, bf16[2,768,768]{2,1,0:T(8,128)(2,1)}, f32[512,768]{1,0:T(8,128)}, f32[8,768]{1,0:T(8,128)}, f32[8...) custom-call(bf16[2,512,768]{2,1,0:T(8,128)(2,1)} %get-tuple-element., ...), custom_call_target="tpu_custom_call" | custom-call | tf_op jit(solution)/shard_map/attention_backward/pallas_call | solution.py:1017
  212.1 62.9 %scatter_gradients.1 = (f32[1,48,1536]{2,1,0:T(8,128)}, f32[1,48,1536]{2,1,0:T(8,128)}, f32[4,48,384]{2,1,0:T(8,128)}, f32[2,48,384]{2,1,0:T(8,128)}, f32[1,48,3...) custom-call(bf16[1,4,48,1536]{3,2,1,0:T(8,128)(2,1)} %get-tuple-element.103.refs_0_, ...), custom_call_target="tpu_custom_call" | custom-call | tf_op jit(solution)/shard_map/scatter_gradients/pallas_call | solution.py:668
  275.0 0.0 copy-start.1
  275.1 0.0 copy-start
  275.1 3.7 %finish.1 = (f32[2,768]{1,0:T(2,128)}, f32[2,768]{1,0:T(2,128)}, f32[2,768]{1,0:T(2,128)}, f32[5,384]{1,0:T(8,128)}, f32[1,1536]{1,0:T(1,128)}, /*index=5*/f32[1...) custom-call(f32[24,768]{1,0:T(8,128)} %get-tuple-element.102.stack, ...), custom_call_target="tpu_custom_call" | custom-call | tf_op jit(solution)/shard_map/finish/pallas_call | solution.py:708
  278.7 1.3 reduce
  280.1 0.0 copy-done.1
  280.1 0.6 copy.34
  280.7 0.0 copy-done
  280.7 0.7 copy.35
Async XLA Ops:
  275.0 5.0 %copy-start.1 = (f32[1,48,384]{2,1,0:T(8,128)S(1)}, f32[1,48,384]{2,1,0:T(8,128)}, u32[]{:S(2)}) copy-start(f32[1,48,384]{2,1,0:T(8,128)} %get-tuple-element.124) | copy-start | bytes 221188
  275.1 5.6 %copy-start = (f32[1,48,1536]{2,1,0:T(8,128)S(1)}, f32[1,48,1536]{2,1,0:T(8,128)}, u32[]{:S(2)}) copy-start(f32[1,48,1536]{2,1,0:T(8,128)} %get-tuple-element.130) | copy-start | bytes 884740

commit v5 on v4

--- a/solution.py
+++ b/solution.py
@@ -261,6 +261,10 @@
             if 0 <= stage < len(lists[index]):
                 order.append(lists[index][stage])
     return order
+
+
+def cuts(counts):
+    return [(i, a, min(2, m)) for i, m in enumerate(counts) for a in range(0, m, 2)]
 
 
 class Share:
@@ -343,8 +347,10 @@
     for share in shares:
         share.start()
     movers = [
-        Gather(place, shards[i], fulls[i], send.at[i], recv.at[i], local.at[i], i < wholes)
-        for i in range(count)
+        Gather(
+            place, shards[i].at[pl.ds(a, m)], fulls[i].at[pl.ds(a, m)], send.at[n], recv.at[n], local.at[n], i < wholes
+        )
+        for n, (i, a, m) in enumerate(cuts([shard.shape[0] for shard in shards]))
     ]
     for mover in movers[:2]:
         mover.stage1()
@@ -357,7 +363,7 @@
             tokens.forward()
         if step.__func__ in (Gather.stage2, Gather.settle):
             landed += 1
-            if landed + 1 < count:
+            if landed + 1 < len(movers):
                 movers[landed + 1].stage1()
     tokens.finish()
     for share in shares:
@@ -369,6 +375,7 @@
     outs = [
         jax.ShapeDtypeStruct((s.shape[0], 4, 2, 2, s.shape[1], 2 * s.shape[2]), BF16) for s in shards
     ]
+    movers = len(cuts([s.shape[0] for s in shards]))
     bias, facts = (16, bias_rows.shape[1]), (8, columns[0].shape[1])
     outs += [
         jax.ShapeDtypeStruct((2,) + rows.shape, rows.dtype),
@@ -381,9 +388,9 @@
         in_specs=[pl.BlockSpec(memory_space=pltpu.VMEM)] * (count + 6),
         out_specs=[pl.BlockSpec(memory_space=pl.ANY)] * (count + 3),
         scratch_shapes=[
-            pltpu.SemaphoreType.DMA((count, 10)),
-            pltpu.SemaphoreType.DMA((count, 10)),
-            pltpu.SemaphoreType.DMA((count,)),
+            pltpu.SemaphoreType.DMA((movers, 10)),
+            pltpu.SemaphoreType.DMA((movers, 10)),
+            pltpu.SemaphoreType.DMA((movers,)),
             pltpu.SemaphoreType.DMA((5,)),
             pltpu.SemaphoreType.DMA((2, 3)),
             pltpu.VMEM(bias, F32),

time: 283 us -> 280 us (0.989)
    pallas_call x1, Pallas kernels: 54.5 us -> 50.4 us  [attention_forward(): pl.pallas_call(functools.partial(forward_kernel, subs), grid=(pairs,), ou...]
where the time goes in v5:
time: 280 us; the launch traced here: 279 us
  Pallas kernels  275 us (98%)
    pallas_call x1, Pallas kernels, scatter_gradients(): pl.pallas_call(functools.partial(scatter_kernel, subs, early, count), out...  63.4 us
    pallas_call x1, Pallas kernels, gather_weights(): pl.pallas_call(functools.partial(gather_kernel, subs, count, wholes), out...  55.8 us
    pallas_call x1, Pallas kernels, attention_backward(): pl.pallas_call(functools.partial(backward_kernel, subs), grid=(pairs + 1,...  53.4 us
    pallas_call x1, Pallas kernels, attention_forward(): pl.pallas_call(functools.partial(forward_kernel, subs), grid=(pairs,), ou...  50.4 us
    pallas_call x1, Pallas kernels, ffn_forward(): pl.pallas_call(functools.partial(ffn_forward_kernel, subs), grid=(units /...  25.6 us
    pallas_call x1, Pallas kernels, ffn_backward(): pl.pallas_call(functools.partial(ffn_backward_kernel, subs), grid=(units...  22.4 us

profile of v5, /device:TPU:0, one launch (start us, length us, event | category | flops | bytes accessed | tf_op | source)
XLA Modules:
  0.0 279.4 jit_solution(8194886337327127904)
XLA Ops:
  0.6 1.3 broadcast_in_dim.24.refs_7_
  1.9 55.8 %gather_weights.1 = (bf16[2,4,2,2,48,768]{5,4,3,2,1,0:T(8,128)(2,1)}, bf16[4,4,2,2,48,768]{5,4,3,2,1,0:T(8,128)(2,1)}, bf16[1,4,2,2,48,768]{5,4,3,2,1,0:T(8,128)...) custom-call(bf16[2,48,384]{2,1,0:T(8,128)(2,1)} %refs_0_.1, ...), custom_call_target="tpu_custom_call" | custom-call | tf_op jit(solution)/shard_map/gather_weights/pallas_call | solution.py:385
  57.8 50.4 %attention_forward.1 = (bf16[768,512]{1,0:T(8,128)(2,1)}, bf16[12,1024,512]{2,1,0:T(8,128)(2,1)}, bf16[512,768]{1,0:T(8,128)(2,1)}, bf16[512,768]{1,0:T(8,128)(2...) custom-call(bf16[2,512,768]{2,1,0:T(8,128)(2,1)} %get-tuple-element., ...), custom_call_target="tpu_custom_call", output_to_operand_aliasing={{6}: (5, {}), {7}: (6, {})} | custom-call | tf_op jit(solution)/shard_map/attention_forward/pallas_call | solution.py:819
  108.1 25.6 %ffn_forward.1 = (bf16[512,3072]{1,0:T(8,128)(2,1)}, bf16[512,3072]{1,0:T(8,128)(2,1)}, bf16[512,768]{1,0:T(8,128)(2,1)}, f32[512,768]{1,0:T(8,128)}, f32[512,1]...) custom-call(bf16[2,512,768]{2,1,0:T(8,128)(2,1)} %get-tuple-element.72.both, ...), custom_call_target="tpu_custom_call" | custom-call | flops 5435817984 | bytes 16908288 | tf_op jit(solution)/shard_map/ffn_forward/pallas_call | solution.py:1155
  133.7 22.4 %ffn_backward.1 = (bf16[768,3072]{1,0:T(8,128)(2,1)}, bf16[768,3072]{1,0:T(8,128)(2,1)}, f32[1,3072]{1,0:T(1,128)}, f32[512,768]{1,0:T(8,128)}, bf16[768,512]{1,...) custom-call(bf16[512,768]{1,0:T(8,128)(2,1)} %get-tuple-element.88.result, ...), custom_call_target="tpu_custom_call" | custom-call | flops 10871635968 | bytes 28704768 | tf_op jit(solution)/shard_map/ffn_backward/pallas_call | solution.py:1246
  156.2 53.4 %attention_backward.1 = (bf16[4,768,768]{2,1,0:T(8,128)(2,1)}, bf16[2,768,768]{2,1,0:T(8,128)(2,1)}, f32[512,768]{1,0:T(8,128)}, f32[8,768]{1,0:T(8,128)}, f32[8...) custom-call(bf16[2,512,768]{2,1,0:T(8,128)(2,1)} %get-tuple-element., ...), custom_call_target="tpu_custom_call" | custom-call | tf_op jit(solution)/shard_map/attention_backward/pallas_call | solution.py:1024
  209.6 63.4 %scatter_gradients.1 = (f32[1,48,1536]{2,1,0:T(8,128)}, f32[1,48,1536]{2,1,0:T(8,128)}, f32[4,48,384]{2,1,0:T(8,128)}, f32[2,48,384]{2,1,0:T(8,128)}, f32[1,48,3...) custom-call(bf16[1,4,48,1536]{3,2,1,0:T(8,128)(2,1)} %get-tuple-element.103.refs_0_, ...), custom_call_target="tpu_custom_call" | custom-call | tf_op jit(solution)/shard_map/scatter_gradients/pallas_call | solution.py:675
  273.0 0.0 copy-start.1
  273.0 0.0 copy-start
  273.0 3.7 %finish.1 = (f32[2,768]{1,0:T(2,128)}, f32[2,768]{1,0:T(2,128)}, f32[2,768]{1,0:T(2,128)}, f32[5,384]{1,0:T(8,128)}, f32[1,1536]{1,0:T(1,128)}, /*index=5*/f32[1...) custom-call(f32[24,768]{1,0:T(8,128)} %get-tuple-element.102.stack, ...), custom_call_target="tpu_custom_call" | custom-call | tf_op jit(solution)/shard_map/finish/pallas_call | solution.py:715
  276.7 1.3 reduce
  278.0 0.0 copy-done.1
  278.0 0.6 copy.34
  278.7 0.0 copy-done
  278.7 0.7 copy.35
Async XLA Ops:
  273.0 5.0 %copy-start.1 = (f32[1,48,384]{2,1,0:T(8,128)S(1)}, f32[1,48,384]{2,1,0:T(8,128)}, u32[]{:S(2)}) copy-start(f32[1,48,384]{2,1,0:T(8,128)} %get-tuple-element.124) | copy-start | bytes 221188
  273.0 5.6 %copy-start = (f32[1,48,1536]{2,1,0:T(8,128)S(1)}, f32[1,48,1536]{2,1,0:T(8,128)}, u32[]{:S(2)}) copy-start(f32[1,48,1536]{2,1,0:T(8,128)} %get-tuple-element.130) | copy-start | bytes 884740

commit v6 on v5

--- a/solution.py
+++ b/solution.py
@@ -762,6 +762,7 @@
     @pl.when(step == 5)
     def _():
         movers[1].stage3()
+        movers[0].stage4()
 
     tokens = both[...].reshape(length, both.shape[2])
     mine = both[place.c]
@@ -801,8 +802,7 @@
 
     @pl.when(step == pl.num_programs(0) - 1)
     def _():
-        for mover in movers:
-            mover.stage4()
+        movers[1].stage4()
         for mover in movers:
             mover.stage5()
 
@@ -913,12 +913,12 @@
     def _():
         small_sum.land(3)
         small_sum.hop(4)
+        movers[0].stage3()
 
     @pl.when(step == 5)
     def _():
         small_sum.land(4)
         sums[...] = running[4]
-        movers[0].stage3()
 
     @pl.when(step < pairs)
     def _():
@@ -1344,7 +1344,7 @@
     sums, bias_sum, input_grad = scatter_gradients(
         subs,
         [down_piece, up_piece],
-        [query_part, kv_part, out_part[None]],
+        [kv_part, query_part, out_part[None]],
         [q_bias, v_bias],
         input_grad,
         input_low,
@@ -1356,7 +1356,7 @@
         ]
         stack = lax.psum(stack, "dp", axis_index_groups=groups)
         bias_sum = lax.psum(bias_sum, "dp", axis_index_groups=groups)
-    down_sum, up_sum, query_sum, kv_sum, out_sum = sums
+    down_sum, up_sum, kv_sum, query_sum, out_sum = sums
     half = ffn_bias.shape[0]
     gains, shifts, out_biases, attn_biases, unit_biases, rms, query_sum, kv_sum, up_sum, input_grad, output = finish(
         subs, rows, stack, bias_sum, cols, half, [query_sum, kv_sum, up_sum, input_grad, output]

time: 280 us -> 280 us (level)
  no operation moved by 1% of the time
where the time goes in v6:
time: 280 us; the launch traced here: 279 us
  Pallas kernels  275 us (98%)
    pallas_call x1, Pallas kernels, scatter_gradients(): pl.pallas_call(functools.partial(scatter_kernel, subs, early, count), out...  62 us
    pallas_call x1, Pallas kernels, gather_weights(): pl.pallas_call(functools.partial(gather_kernel, subs, count, wholes), out...  55.8 us
    pallas_call x1, Pallas kernels, attention_backward(): pl.pallas_call(functools.partial(backward_kernel, subs), grid=(pairs + 1,...  54.8 us
    pallas_call x1, Pallas kernels, attention_forward(): pl.pallas_call(functools.partial(forward_kernel, subs), grid=(pairs,), ou...  50.4 us
    pallas_call x1, Pallas kernels, ffn_forward(): pl.pallas_call(functools.partial(ffn_forward_kernel, subs), grid=(units /...  25.6 us
    pallas_call x1, Pallas kernels, ffn_backward(): pl.pallas_call(functools.partial(ffn_backward_kernel, subs), grid=(units...  22.4 us

profile of v6, /device:TPU:0, one launch (start us, length us, event | category | flops | bytes accessed | tf_op | source)
XLA Modules:
  0.0 279.3 jit_solution(6727091294252770842)
XLA Ops:
  0.6 1.3 broadcast_in_dim.24.refs_7_
  1.9 55.8 %gather_weights.1 = (bf16[2,4,2,2,48,768]{5,4,3,2,1,0:T(8,128)(2,1)}, bf16[4,4,2,2,48,768]{5,4,3,2,1,0:T(8,128)(2,1)}, bf16[1,4,2,2,48,768]{5,4,3,2,1,0:T(8,128)...) custom-call(bf16[2,48,384]{2,1,0:T(8,128)(2,1)} %refs_0_.1, ...), custom_call_target="tpu_custom_call" | custom-call | tf_op jit(solution)/shard_map/gather_weights/pallas_call | solution.py:385
  57.8 50.4 %attention_forward.1 = (bf16[768,512]{1,0:T(8,128)(2,1)}, bf16[12,1024,512]{2,1,0:T(8,128)(2,1)}, bf16[512,768]{1,0:T(8,128)(2,1)}, bf16[512,768]{1,0:T(8,128)(2...) custom-call(bf16[2,512,768]{2,1,0:T(8,128)(2,1)} %get-tuple-element., ...), custom_call_target="tpu_custom_call", output_to_operand_aliasing={{6}: (5, {}), {7}: (6, {})} | custom-call | tf_op jit(solution)/shard_map/attention_forward/pallas_call | solution.py:819
  108.1 25.6 %ffn_forward.1 = (bf16[512,3072]{1,0:T(8,128)(2,1)}, bf16[512,3072]{1,0:T(8,128)(2,1)}, bf16[512,768]{1,0:T(8,128)(2,1)}, f32[512,768]{1,0:T(8,128)}, f32[512,1]...) custom-call(bf16[2,512,768]{2,1,0:T(8,128)(2,1)} %get-tuple-element.72.both, ...), custom_call_target="tpu_custom_call" | custom-call | flops 5435817984 | bytes 16908288 | tf_op jit(solution)/shard_map/ffn_forward/pallas_call | solution.py:1155
  133.7 22.4 %ffn_backward.1 = (bf16[768,3072]{1,0:T(8,128)(2,1)}, bf16[768,3072]{1,0:T(8,128)(2,1)}, f32[1,3072]{1,0:T(1,128)}, f32[512,768]{1,0:T(8,128)}, bf16[768,512]{1,...) custom-call(bf16[512,768]{1,0:T(8,128)(2,1)} %get-tuple-element.88.result, ...), custom_call_target="tpu_custom_call" | custom-call | flops 10871635968 | bytes 28704768 | tf_op jit(solution)/shard_map/ffn_backward/pallas_call | solution.py:1246
  156.2 54.8 %attention_backward.1 = (bf16[4,768,768]{2,1,0:T(8,128)(2,1)}, bf16[2,768,768]{2,1,0:T(8,128)(2,1)}, f32[512,768]{1,0:T(8,128)}, f32[8,768]{1,0:T(8,128)}, f32[8...) custom-call(bf16[2,512,768]{2,1,0:T(8,128)(2,1)} %get-tuple-element., ...), custom_call_target="tpu_custom_call" | custom-call | tf_op jit(solution)/shard_map/attention_backward/pallas_call | solution.py:1024
  211.0 62.0 %scatter_gradients.1 = (f32[1,48,1536]{2,1,0:T(8,128)}, f32[1,48,1536]{2,1,0:T(8,128)}, f32[2,48,384]{2,1,0:T(8,128)}, f32[4,48,384]{2,1,0:T(8,128)}, f32[1,48,3...) custom-call(bf16[1,4,48,1536]{3,2,1,0:T(8,128)(2,1)} %get-tuple-element.103.refs_0_, ...), custom_call_target="tpu_custom_call" | custom-call | tf_op jit(solution)/shard_map/scatter_gradients/pallas_call | solution.py:675
  272.9 0.0 copy-start.1
  272.9 0.0 copy-start
  272.9 3.7 %finish.1 = (f32[2,768]{1,0:T(2,128)}, f32[2,768]{1,0:T(2,128)}, f32[2,768]{1,0:T(2,128)}, f32[5,384]{1,0:T(8,128)}, f32[1,1536]{1,0:T(1,128)}, /*index=5*/f32[1...) custom-call(f32[24,768]{1,0:T(8,128)} %get-tuple-element.102.stack, ...), custom_call_target="tpu_custom_call" | custom-call | tf_op jit(solution)/shard_map/finish/pallas_call | solution.py:715
  276.6 1.3 reduce
  277.9 0.0 copy-done.1
  277.9 0.6 copy.34
  278.6 0.0 copy-done
  278.6 0.7 copy.35
Async XLA Ops:
  272.9 5.0 %copy-start.1 = (f32[1,48,384]{2,1,0:T(8,128)S(1)}, f32[1,48,384]{2,1,0:T(8,128)}, u32[]{:S(2)}) copy-start(f32[1,48,384]{2,1,0:T(8,128)} %get-tuple-element.124) | copy-start | bytes 221188
  272.9 5.6 %copy-start = (f32[1,48,1536]{2,1,0:T(8,128)S(1)}, f32[1,48,1536]{2,1,0:T(8,128)}, u32[]{:S(2)}) copy-start(f32[1,48,1536]{2,1,0:T(8,128)} %get-tuple-element.130) | copy-start | bytes 884740
